TPU v7x, 32 devices: a whole 2x2x4 slice. The times are simulated.
32 devices in a mesh: groups: 2 (over x), dp: 8 (over z, y), tensor: 2 (over core).
Axes of the slice: x: 2, y: 2, z: 4, core: 2. Of those that a mesh axis runs over, the one named last changes fastest.
Arguments:
- step_input: bfloat16 [1024, 4, 8192], P(('groups', 'dp'), None, 'tensor'), parts along dimension 0, may hold values from -8 to 8
- new_kv: bfloat16 [1024, 4, 2, 1024], P(('groups', 'dp'), None, None, 'tensor'), parts along dimension 0, may hold values from -24 to 24
- resp_cache: bfloat16 [1024, 8, 2, 1024], P(('groups', 'dp'), None, None, 'tensor'), parts along dimension 0, may hold values from -24 to 24
- policy_prompt: bfloat16 [16, 128, 2, 1024], P(('groups', 'dp'), None, None, 'tensor'), parts along dimension 0, may hold values from -24 to 24
- ref_prompt: bfloat16 [16, 128, 2, 1024], P(('groups', 'dp'), None, None, 'tensor'), parts along dimension 0, may hold values from -24 to 24
- prompt_len: int32 [16], P(('groups', 'dp')), parts along dimension 0, may hold values from 1 to 128
- resp_len: int32 [1024], P(('groups', 'dp')), parts along dimension 0, may hold values from 1 to 8
- row_owner: int32 [1024], P(('groups', 'dp')), parts along dimension 0, may hold values from 0 to 7, as said below
- finished: int32 [1024], P(('groups', 'dp')), parts along dimension 0, may hold values 0 or 1
- probe: float32 [8192], P('tensor'), may hold values from -0.12 to 0.12
Outputs:
- decoded: bfloat16 [1024, 4, 8192], P(('groups', 'dp'), None, 'tensor'), parts along dimension 0
- ref_score: float32 [16, 64, 4], P(('groups', 'dp')), parts along dimension 0
There are 2 independent parts, one for each index of `groups`. A program takes and returns all parts, laid end to end along the dimension named above; an argument that names none is the same for every part. Nothing has to cross between parts.
Inputs may be any that keep to these rules, and one draw needn't show every extreme that they name: `row_owner`: among the rows of one block at most 8 name the same owner; in every draw one owner is named by exactly 8 rows of every block.
All inputs are finite; a program needn't handle non-finite values. No bound on the sum of `finished` on one device may be relied on, other than what follows from the above.
Results may differ from a plain program's by a relative error of at most 0.012.
The roundings to bfloat16 on the way count: a program that leaves them out, or rounds other values in their place, can miss the bound.
Values may be sent and summed in bfloat16 or wider, within the bound.
No kernel may reach another device: no remote copies, remote signals or barrier semaphores. Data moves between devices by JAX's collectives and lax.ppermute only.
A program may use at most 128 MiB of HBM per device.

v0:
```python
import math

import jax
import jax.numpy as jnp
from jax import lax
from jax.experimental import pallas as pl
from jax.experimental.pallas import tpu as pltpu
from jax.sharding import PartitionSpec as P

HD = 128


def softmax_pieces(scores, key_valid):
    masked = jnp.where(key_valid, scores, -jnp.inf)
    top_score = jnp.max(masked, axis=-1, keepdims=True)
    weight = jnp.exp(masked - top_score)
    return (weight, jnp.sum(weight, axis=-1), top_score[..., 0])


def per_device(
    step_input,
    new_kv,
    resp_cache,
    policy_prompt,
    ref_prompt,
    prompt_len,
    resp_len,
    row_owner,
    finished,
    probe,
):
    row_count = step_input.shape[0]
    step_count = step_input.shape[1]
    q_width = step_input.shape[2]
    kv_width = new_kv.shape[3]
    q_heads = q_width // HD
    kv_heads = kv_width // HD
    group_size = q_heads // kv_heads
    inv_scale = 1.0 / math.sqrt(HD)
    peer_count = lax.axis_size("dp")
    capacity = max(2, (row_count + peer_count - 1) // peer_count)
    slot_count = peer_count * capacity
    resp_slots = resp_cache.shape[1]
    prompt_width = policy_prompt.shape[1]
    row_iota = jnp.arange(row_count, dtype=jnp.int32)
    same_owner = (row_owner[:, None] == row_owner[None, :]) & (
        row_iota[None, :] < row_iota[:, None]
    )
    slot_index = row_owner * capacity + jnp.sum(same_owner.astype(jnp.int32), axis=1)
    dispatch = slot_index[:, None] == jnp.arange(slot_count, dtype=jnp.int32)[None, :]
    slot_used = jnp.any(dispatch, axis=0)
    slot_row = jnp.sum(jnp.where(dispatch, row_iota[:, None], 0), axis=0)

    def to_slots(rows_data):
        picked = jnp.take(rows_data, slot_row, axis=0)
        mask_shape = (slot_count,) + (1,) * (rows_data.ndim - 1)
        picked = jnp.where(slot_used.reshape(mask_shape), picked, jnp.zeros_like(picked))
        return picked.reshape((peer_count, capacity) + rows_data.shape[1:])

    live_len = jnp.where(finished == 1, resp_len, 0).astype(jnp.bfloat16)
    own_all = jnp.concatenate([resp_cache, new_kv], axis=1)
    reply_iota = jnp.arange(resp_slots + step_count)
    pol_keys = policy_prompt[0, :, 0].reshape(prompt_width, kv_heads, HD)
    pol_values = policy_prompt[0, :, 1].reshape(prompt_width, kv_heads, HD)
    prompt_valid = jnp.arange(prompt_width) < prompt_len[0]
    resp_keys = own_all[:, :, 0].reshape(row_count, -1, kv_heads, HD)
    resp_values = own_all[:, :, 1].reshape(row_count, -1, kv_heads, HD)
    previous = jnp.zeros((row_count, q_width), jnp.float32)
    decoded_list = []
    kept_list = []
    for step_idx in range(step_count):
        queries = (step_input[:, step_idx].astype(jnp.float32) + previous).astype(jnp.bfloat16)
        received = lax.all_to_all(to_slots(queries), "dp", split_axis=0, concat_axis=0, tiled=True)
        lead_shape = received.shape[:2]
        prompt_queries = received.reshape(-1, kv_heads, group_size, HD)
        scores = (
            jnp.einsum(
                "skgd,tkd->skgt", prompt_queries, pol_keys, preferred_element_type=jnp.float32
            )
            * inv_scale
        )
        prompt_weight, prompt_weight_sum, prompt_top_score = softmax_pieces(scores, prompt_valid)
        prompt_summed = jnp.einsum(
            "skgt,tkd->skgd",
            prompt_weight.astype(jnp.bfloat16),
            pol_values,
            preferred_element_type=jnp.float32,
        )
        part_out = (
            (prompt_summed / prompt_weight_sum[..., None])
            .astype(jnp.bfloat16)
            .reshape(lead_shape + (q_width,))
        )
        part_lse = (prompt_top_score + jnp.log(prompt_weight_sum)).reshape(lead_shape + (q_heads,))
        back_out = lax.all_to_all(part_out, "dp", split_axis=0, concat_axis=0, tiled=True)
        back_lse = lax.all_to_all(part_lse, "dp", split_axis=0, concat_axis=0, tiled=True)
        results = (back_out, back_lse, received)
        back_out = results[0]
        back_lse = results[1]
        kept_list.append(results[2])
        prompt_out = jnp.take(back_out.reshape(slot_count, q_width), slot_index, axis=0).astype(
            jnp.float32
        )
        prompt_lse = jnp.take(back_lse.reshape(slot_count, q_heads), slot_index, axis=0)
        query_heads = queries.reshape(row_count, kv_heads, group_size, HD)
        scores = (
            jnp.einsum(
                "rkgd,rtkd->rkgt", query_heads, resp_keys, preferred_element_type=jnp.float32
            )
            * inv_scale
        )
        reply_valid = jnp.where(
            reply_iota[None, :] < resp_slots,
            reply_iota[None, :] < resp_len[:, None],
            reply_iota[None, :] <= resp_slots + step_idx,
        )
        weight, weight_sum, top_score = softmax_pieces(scores, reply_valid[:, None, None, :])
        summed = jnp.einsum(
            "rkgt,rtkd->rkgd",
            weight.astype(jnp.bfloat16),
            resp_values,
            preferred_element_type=jnp.float32,
        )
        own_out = (summed / weight_sum[..., None]).reshape(row_count, q_heads, HD)
        own_lse = (top_score + jnp.log(weight_sum)).reshape(row_count, q_heads)
        joint_lse = jnp.maximum(prompt_lse, own_lse)
        prompt_wt = jnp.exp(prompt_lse - joint_lse)
        own_wt = jnp.exp(own_lse - joint_lse)
        blended = (
            prompt_wt[..., None] * prompt_out.reshape(row_count, q_heads, HD)
            + own_wt[..., None] * own_out
        ) / (prompt_wt + own_wt)[..., None]
        decoded_now = blended.reshape(row_count, q_width).astype(jnp.bfloat16)
        decoded_list.append(decoded_now)
        previous = lax.optimization_barrier(decoded_now).astype(jnp.float32)
    recv_kv, recv_live = (
        lax.all_to_all(to_slots(own_all), "dp", split_axis=0, concat_axis=0, tiled=True),
        lax.all_to_all(to_slots(live_len), "dp", split_axis=0, concat_axis=0, tiled=True),
    )
    recv_queries = jnp.stack(kept_list, axis=2)
    ref_keys = ref_prompt[0, :, 0].reshape(prompt_width, kv_heads, HD)
    ref_values = ref_prompt[0, :, 1].reshape(prompt_width, kv_heads, HD)
    slot_kv = recv_kv.reshape(slot_count, resp_slots + step_count, 2, kv_width)
    slot_keys = slot_kv[:, :, 0].reshape(slot_count, -1, kv_heads, HD)
    slot_values = slot_kv[:, :, 1].reshape(slot_count, -1, kv_heads, HD)
    slot_len = recv_live.reshape(slot_count).astype(jnp.int32)
    slot_queries = recv_queries.reshape(slot_count, step_count, q_width)
    probe_heads = probe.reshape(kv_heads, group_size, HD)
    prompt_mask = jnp.broadcast_to(prompt_valid[None, :], (slot_count, prompt_width))
    score_list = []
    for step_idx in range(step_count):
        queries = slot_queries[:, step_idx].reshape(slot_count, kv_heads, group_size, HD)
        prompt_scores = (
            jnp.einsum("skgd,tkd->skgt", queries, ref_keys, preferred_element_type=jnp.float32)
            * inv_scale
        )
        reply_scores = (
            jnp.einsum("skgd,stkd->skgt", queries, slot_keys, preferred_element_type=jnp.float32)
            * inv_scale
        )
        reply_valid = jnp.where(
            reply_iota[None, :] < resp_slots,
            reply_iota[None, :] < slot_len[:, None],
            reply_iota[None, :] <= resp_slots + step_idx,
        )
        key_valid = jnp.concatenate([prompt_mask, reply_valid], axis=1)
        weight, weight_sum, top_score = softmax_pieces(
            jnp.concatenate([prompt_scores, reply_scores], axis=-1), key_valid[:, None, None, :]
        )
        weight_low = weight.astype(jnp.bfloat16)
        summed = jnp.einsum(
            "skgt,tkd->skgd",
            weight_low[..., :prompt_width],
            ref_values,
            preferred_element_type=jnp.float32,
        )
        summed = summed + jnp.einsum(
            "skgt,stkd->skgd",
            weight_low[..., prompt_width:],
            slot_values,
            preferred_element_type=jnp.float32,
        )
        ref_out = summed / weight_sum[..., None]
        score_list.append(
            jnp.einsum("skgd,kgd->s", ref_out, probe_heads, precision=lax.Precision.HIGHEST)
        )
    head_terms = jnp.stack(score_list, axis=1)
    head_total = lax.psum(head_terms, "tensor")
    ref_score = jnp.where(slot_len[:, None] > 0, head_total, jnp.zeros((), jnp.float32)).reshape(
        1, slot_count, step_count
    )
    return (jnp.stack(decoded_list, axis=1), ref_score)


def ring_order(count):
    return list(range(0, count, 2)) + list(range(count - 1, 0, -2))


def iota(shape, dim):
    return lax.broadcasted_iota(jnp.int32, shape, dim)


def split_matrix(pairs):
    i = iota((2 * pairs, 2 * pairs), 0)
    j = iota((2 * pairs, 2 * pairs), 1)
    src = jnp.where(i < pairs, 2 * i, 2 * (i - pairs) + 1)
    return jnp.where(src == j, 1.0, 0.0).astype(jnp.bfloat16)


def swap_matrix(outer, inner):
    n = outer * inner
    i = iota((n, n), 0)
    j = iota((n, n), 1)
    src = (i % outer) * inner + i // outer
    return jnp.where(src == j, 1.0, 0.0).astype(jnp.bfloat16)


def mm(a, b):
    return jnp.dot(a, b, preferred_element_type=jnp.float32)


def mm_t(a, b):
    return lax.dot_general(a, b, (((1,), (1,)), ((), ())), preferred_element_type=jnp.float32)


def slots_kernel(owner_ref, len_ref, fin_ref, slot_ref, count_ref):
    peers = count_ref.shape[0]
    slots = slot_ref.shape[1]
    capacity = slots // peers
    for i in range(slots):
        slot_ref[0, i] = -1
        slot_ref[1, i] = 1
        slot_ref[2, i] = 0
    for o in range(peers):
        count_ref[o] = 0

    def place(r, c):
        o = jnp.clip(owner_ref[r], 0, peers - 1)
        k = count_ref[o]
        at = o * capacity + jnp.minimum(k, capacity - 1)
        slot_ref[0, at] = r
        slot_ref[1, at] = len_ref[r]
        slot_ref[2, at] = fin_ref[r]
        count_ref[o] = k + 1
        return c

    lax.fori_loop(0, owner_ref.shape[0], place, 0, unroll=4)


def slot_tables(row_owner, resp_len, finished, peers, capacity):
    smem = pl.BlockSpec(memory_space=pltpu.SMEM)
    return pl.pallas_call(
        slots_kernel,
        in_specs=[smem] * 3,
        out_specs=smem,
        out_shape=jax.ShapeDtypeStruct((3, peers * capacity), jnp.int32),
        scratch_shapes=[pltpu.SMEM((peers,), jnp.int32)],
        name="slots",
    )(row_owner, resp_len, finished)


def prep_kernel(slot_ref, x_hbm, rc_hbm, nk_hbm, xs_ref, ko_ref, vo_ref, xbuf, rcbuf, nkbuf, sem):
    peers, width, kv_width = ko_ref.shape
    _, capacity, old, _, _ = rcbuf.shape
    steps = nkbuf.shape[2]
    flights = []
    for o in range(peers):
        flight = []
        for k in range(capacity):
            row = jnp.maximum(slot_ref[0, o * capacity + k], 0)
            flight += [
                pltpu.make_async_copy(x_hbm.at[row], xbuf.at[o, k], sem.at[o, k, 0]),
                pltpu.make_async_copy(rc_hbm.at[row], rcbuf.at[o, k], sem.at[o, k, 1]),
                pltpu.make_async_copy(nk_hbm.at[row], nkbuf.at[o, k], sem.at[o, k, 2]),
            ]
        for c in flight:
            c.start()
        flights.append(flight)
    n_old, n_new = capacity * old, capacity * steps
    split_rc = split_matrix(n_old)
    split_nk = split_matrix(n_new)
    to_steps = swap_matrix(capacity, steps)
    zero = jnp.zeros((width - n_old - n_new, kv_width), jnp.float32)
    for o in range(peers):
        for c in flights[o]:
            c.wait()
        rc = mm(split_rc, rcbuf[o].reshape(2 * n_old, kv_width))
        nk = mm(split_nk, nkbuf[o].reshape(2 * n_new, kv_width))
        ko_ref[o] = jnp.concatenate([rc[:n_old], nk[:n_new], zero], 0).astype(jnp.bfloat16)
        vo_ref[o] = jnp.concatenate([rc[n_old:], nk[n_new:], zero], 0).astype(jnp.bfloat16)
        xs_ref[o] = mm(to_steps, xbuf[o].reshape(n_new, -1)).astype(jnp.bfloat16)


def prepare(slots, x, rc, nk, peers, capacity, width):
    _, steps, q_width = x.shape
    old = rc.shape[1]
    kv_width = rc.shape[3]
    smem = pl.BlockSpec(memory_space=pltpu.SMEM)
    vmem = pl.BlockSpec(memory_space=pltpu.VMEM)
    anyspec = pl.BlockSpec(memory_space=pl.ANY)
    bf = jnp.bfloat16
    return pl.pallas_call(
        prep_kernel,
        in_specs=[smem] + [anyspec] * 3,
        out_specs=[vmem] * 3,
        out_shape=[
            jax.ShapeDtypeStruct((peers, steps * capacity, q_width), bf),
            jax.ShapeDtypeStruct((peers, width, kv_width), bf),
            jax.ShapeDtypeStruct((peers, width, kv_width), bf),
        ],
        scratch_shapes=[
            pltpu.VMEM((peers, capacity, steps, q_width), bf),
            pltpu.VMEM((peers, capacity, old, 2, kv_width), bf),
            pltpu.VMEM((peers, capacity, steps, 2, kv_width), bf),
            pltpu.SemaphoreType.DMA((peers, capacity, 3)),
        ],
        compiler_params=pltpu.CompilerParams(vmem_limit_bytes=24 << 20),
        cost_estimate=pl.CostEstimate(flops=0, transcendentals=0, bytes_accessed=12 << 20),
        name="prep",
    )(slots, x, rc, nk)


def own_masks(slot_ref, base, rows, old, steps, width):
    lane = iota((rows, width), 1)
    sub = iota((rows, width), 0)
    split = rows * old
    is_old = lane < split
    key_row = jnp.where(is_old, lane // old, (lane - split) // steps)
    key_pos = jnp.where(is_old, lane % old, (lane - split) % steps)
    limit = jnp.zeros((rows, width), jnp.int32)
    for k in range(rows):
        limit = jnp.where(sub == k, slot_ref[1, base + k], limit)
    mine = (key_row == sub) & (lane < rows * (old + steps))
    return [
        mine & (key_pos < jnp.where(is_old, limit, step_idx + 1)) for step_idx in range(steps)
    ]


def make_work(pieces, begin, last, earlier, capacity, steps, old, kv_heads, group):
    head_rows = group * capacity
    inv_scale = 1.0 / math.sqrt(HD)
    first = begin == 0

    def body(*refs):
        refs = list(refs)
        me_ref, table_ref, plen_ref, slot_ref = refs[:4]
        xs_hbm, ko_hbm, vo_hbm, probe_ref = refs[4:8]
        refs = refs[8:]
        pols, refs = refs[:pieces], refs[pieces:]
        rfs, refs = refs[:pieces], refs[pieces:]
        if not first:
            refs = refs[1:]
        olds, refs = refs[:earlier], refs[earlier:]
        dec_hbm, score_ref = refs[:2]
        polbuf, refbuf, xs, kc, vp, vr, obuf, insem, outsem = refs[2:]
        width = kc.shape[1] // 3
        kv_width = kv_heads * HD
        me = me_ref[0]
        owners = [table_ref[me, begin + p] for p in range(pieces)]
        loads = []
        for p in range(pieces):
            o = owners[p]
            loads.append(
                [
                    pltpu.make_async_copy(pols[p].at[0], polbuf.at[p], insem.at[p, 0]),
                    pltpu.make_async_copy(rfs[p].at[0], refbuf.at[p], insem.at[p, 1]),
                    pltpu.make_async_copy(xs_hbm.at[o], xs.at[p], insem.at[p, 2]),
                    pltpu.make_async_copy(
                        ko_hbm.at[o], kc.at[p, pl.ds(width, width)], insem.at[p, 3]
                    ),
                    pltpu.make_async_copy(
                        vo_hbm.at[o], vr.at[p, pl.ds(width, width)], insem.at[p, 4]
                    ),
                ]
            )
        for load in loads:
            for c in load:
                c.start()
        split_p = split_matrix(width)
        to_rows = swap_matrix(steps, capacity)
        masks = [
            own_masks(slot_ref, owners[p] * capacity, capacity, old, steps, width)
            for p in range(pieces)
        ]
        lane = iota((head_rows, width), 1)
        pmask = [lane < plen_ref[0 if first else owners[p]] for p in range(pieces)]
        weights = [
            jnp.concatenate(
                [
                    jnp.broadcast_to(
                        probe_ref[g * group + h : g * group + h + 1, :], (capacity, HD)
                    )
                    for h in range(group)
                ],
                0,
            )
            for g in range(kv_heads)
        ]
        for p in range(pieces):
            for c in loads[p]:
                c.wait()
            both = mm(split_p, polbuf[p].reshape(2 * width, kv_width)).astype(jnp.bfloat16)
            kc[p, :width] = both[:width]
            vp[p] = both[width:]
            both = mm(split_p, refbuf[p].reshape(2 * width, kv_width)).astype(jnp.bfloat16)
            kc[p, 2 * width :] = both[:width]
            vr[p, :width] = both[width:]
        prev = [[None] * kv_heads for _ in range(pieces)]
        done = [[None] * steps for _ in range(pieces)]
        totals = [[None] * steps for _ in range(pieces)]
        for s in range(steps):
            for p in range(pieces):
                omask = jnp.concatenate([masks[p][s]] * group, 0)
                x = xs[p, s * capacity : (s + 1) * capacity, :].astype(jnp.float32)
                parts = []
                total = jnp.zeros((head_rows, HD), jnp.float32)
                for g in range(kv_heads):
                    at = slice(g * HD, (g + 1) * HD)
                    q = jnp.concatenate(
                        [x[:, (g * group + h) * HD : (g * group + h + 1) * HD] for h in range(group)],
                        0,
                    )
                    if s > 0:
                        q = q + prev[p][g]
                    q = q.astype(jnp.bfloat16)
                    z = mm_t(q, kc[p, :, at]) * inv_scale
                    zp = jnp.where(pmask[p], z[:, :width], -jnp.inf)
                    zo = jnp.where(omask, z[:, width : 2 * width], -jnp.inf)
                    zr = jnp.where(pmask[p], z[:, 2 * width :], -jnp.inf)
                    top_p = jnp.max(zp, axis=1, keepdims=True)
                    top_o = jnp.max(zo, axis=1, keepdims=True)
                    wp = jnp.exp(zp - top_p)
                    wo = jnp.exp(zo - top_o)
                    lp = jnp.sum(wp, axis=1, keepdims=True)
                    lo = jnp.sum(wo, axis=1, keepdims=True)
                    accp = mm(wp.astype(jnp.bfloat16), vp[p, :, at])
                    acco = mm(wo.astype(jnp.bfloat16), vr[p, width:, at])
                    out_p = (accp * (1.0 / lp)).astype(jnp.bfloat16).astype(jnp.float32)
                    top = jnp.maximum(top_p, top_o)
                    a = lp * jnp.exp(top_p - top)
                    c = jnp.exp(top_o - top)
                    inv = 1.0 / (a + lo * c)
                    mix = out_p * (a * inv) + acco * (c * inv)
                    mix = mix.astype(jnp.bfloat16).astype(jnp.float32)
                    prev[p][g] = mix
                    parts += [mix[h * capacity : (h + 1) * capacity] for h in range(group)]
                    top_r = jnp.maximum(jnp.max(zr, axis=1, keepdims=True), top_o)
                    wr = jnp.exp(zr - top_r)
                    wro = jnp.exp(zo - top_r)
                    lr = jnp.sum(wr + wro, axis=1, keepdims=True)
                    acc = mm(
                        jnp.concatenate([wr.astype(jnp.bfloat16), wro.astype(jnp.bfloat16)], 1),
                        vr[p, :, at],
                    )
                    total = total + (acc * (1.0 / lr)) * weights[g]
                done[p][s] = jnp.concatenate(parts, 1)
                fold = total[:capacity]
                for h in range(1, group):
                    fold = fold + total[h * capacity : (h + 1) * capacity]
                totals[p][s] = fold
        for p in range(pieces):
            d = jnp.concatenate(done[p], 0).astype(jnp.bfloat16)
            obuf[p] = mm(to_rows, d).astype(jnp.bfloat16).reshape(obuf.shape[1:])
            for k in range(capacity):
                row = slot_ref[0, owners[p] * capacity + k]

                @pl.when(row >= 0)
                def _():
                    pltpu.make_async_copy(obuf.at[p, k], dec_hbm.at[row], outsem.at[p, k]).start()

        out_lane = iota((capacity, HD), 1)
        out_sub = iota((capacity, HD), 0)
        for p in range(pieces):
            live = jnp.zeros((capacity, HD), jnp.int32)
            for k in range(capacity):
                live = jnp.where(out_sub == k, slot_ref[2, owners[p] * capacity + k], live)
            here = (out_lane == me * capacity + out_sub) & (live == 1)
            rows = []
            for s in range(steps):
                value = jnp.sum(totals[p][s], axis=1, keepdims=True)
                rows.append(jnp.sum(jnp.where(here, value, 0.0), axis=0, keepdims=True))
            rows = jnp.concatenate(rows, 0)
            if last:
                for t in range(score_ref.shape[1]):
                    score_ref[owners[p], t] = rows
            else:
                score_ref[p] = rows
        if last:
            n = 0
            for part in olds:
                for i in range(part.shape[0]):
                    for t in range(score_ref.shape[1]):
                        score_ref[table_ref[me, n], t] = part[i]
                    n += 1
        for p in range(pieces):
            for k in range(capacity):
                row = slot_ref[0, owners[p] * capacity + k]

                @pl.when(row >= 0)
                def _():
                    pltpu.make_async_copy(obuf.at[p, k], dec_hbm.at[row], outsem.at[p, k]).wait()

    return body


def work_pieces(me, table, plen, slots, prep, probe, pols, rfs, dec, olds, shape, begin, last, old, halves):
    pieces = len(pols)
    first = begin == 0
    xs, ko, vo = prep
    _, steps, q_width = shape
    peers, width, kv_width = ko.shape
    capacity = xs.shape[1] // steps
    kv_heads = kv_width // HD
    group = q_width // kv_width
    body = make_work(pieces, begin, last, len(olds), capacity, steps, old, kv_heads, group)
    smem = pl.BlockSpec(memory_space=pltpu.SMEM)
    vmem = pl.BlockSpec(memory_space=pltpu.VMEM)
    anyspec = pl.BlockSpec(memory_space=pl.ANY)
    args = [me, table, plen, slots, xs, ko, vo, probe, *pols, *rfs]
    specs = [smem] * 4 + [anyspec] * 3 + [vmem] + [anyspec] * (2 * pieces)
    alias = {}
    if not first:
        alias = {len(args): 0}
        args.append(dec)
        specs.append(anyspec)
    args += olds
    specs += [vmem] * len(olds)
    bf = jnp.bfloat16
    scores = (peers, halves, steps, HD) if last else (pieces, steps, HD)
    return pl.pallas_call(
        body,
        in_specs=specs,
        out_specs=[anyspec, vmem],
        out_shape=[
            jax.ShapeDtypeStruct(shape, bf),
            jax.ShapeDtypeStruct(scores, jnp.float32),
        ],
        scratch_shapes=[
            pltpu.VMEM((pieces, width, 2, kv_width), bf),
            pltpu.VMEM((pieces, width, 2, kv_width), bf),
            pltpu.VMEM((pieces, capacity * steps, q_width), bf),
            pltpu.VMEM((pieces, 3 * width, kv_width), bf),
            pltpu.VMEM((pieces, width, kv_width), bf),
            pltpu.VMEM((pieces, 2 * width, kv_width), bf),
            pltpu.VMEM((pieces, capacity, steps, q_width), bf),
            pltpu.SemaphoreType.DMA((pieces, 5)),
            pltpu.SemaphoreType.DMA((pieces, capacity)),
        ],
        input_output_aliases=alias,
        compiler_params=pltpu.CompilerParams(vmem_limit_bytes=24 << 20),
        cost_estimate=pl.CostEstimate(flops=0, transcendentals=0, bytes_accessed=16 << 20),
        name="work",
    )(*args)


def ring_fits(step_input, new_kv, resp_cache, policy_prompt, *rest):
    peers = lax.axis_size("dp")
    row_count, step_count, q_width = step_input.shape
    old = resp_cache.shape[1]
    kv_width = new_kv.shape[3]
    width = policy_prompt.shape[1]
    capacity = max(2, (row_count + peers - 1) // peers)
    gathered = 2 * peers * policy_prompt.size
    exchanged = 2 * step_input.size + new_kv.size + resp_cache.size
    return (
        gathered <= exchanged
        and peers % 2 == 0
        and peers >= 4
        and capacity % 8 == 0
        and peers * capacity <= HD
        and capacity * (old + step_count) <= width
        and width % HD == 0
        and q_width % kv_width == 0
    )


def per_device_ring(
    step_input,
    new_kv,
    resp_cache,
    policy_prompt,
    ref_prompt,
    prompt_len,
    resp_len,
    row_owner,
    finished,
    probe,
):
    row_count, step_count, q_width = step_input.shape
    peers = lax.axis_size("dp")
    halves = lax.axis_size("tensor")
    width = policy_prompt.shape[1]
    capacity = max(2, (row_count + peers - 1) // peers)
    old = resp_cache.shape[1]
    ring = ring_order(peers)
    forward = [(ring[i], ring[(i + 1) % peers]) for i in range(peers)]
    backward = [(b, a) for a, b in forward]
    spot = {d: i for i, d in enumerate(ring)}
    offsets = [0]
    for d in range(1, peers // 2):
        offsets += [-d, d]
    offsets.append(peers // 2)
    table = [[ring[(spot[dev] + off) % peers] for off in offsets] for dev in range(peers)]
    table = jnp.array(table, jnp.int32)
    me = lax.axis_index("dp").astype(jnp.int32).reshape(1)
    probe_heads = probe.reshape(q_width // HD, HD)

    def hop(value, pairs):
        return lax.ppermute(value, "dp", pairs)

    pf = hop(policy_prompt, forward)
    pb = hop(policy_prompt, backward)
    rf = hop(ref_prompt, forward)
    rb = hop(ref_prompt, backward)
    plen_all = lax.all_to_all(
        jnp.broadcast_to(prompt_len, (peers,)), "dp", split_axis=0, concat_axis=0, tiled=True
    )
    slots = slot_tables(row_owner, resp_len, finished, peers, capacity)
    prep = prepare(slots, step_input, resp_cache, new_kv, peers, capacity, width)

    def work(pols, rfs, dec, olds, begin, last=False):
        plen = prompt_len if begin == 0 else plen_all
        return work_pieces(
            me, table, plen, slots, prep, probe_heads, pols, rfs, dec, olds,
            step_input.shape, begin, last, old, halves,
        )

    dec, score = work([policy_prompt], [ref_prompt], None, [], 0)
    scores = [score]
    begin = 1
    for d in range(1, peers // 2):
        now = [pf, pb], [rf, rb]
        pf = hop(pf, forward)
        if d + 1 < peers // 2:
            pb = hop(pb, backward)
            rf = hop(rf, forward)
        rb = hop(rb, backward)
        dec, score = work(*now, dec, [], begin)
        scores.append(score)
        begin += 2
    dec, send = work([pf], [rb], dec, scores, begin, True)
    got = lax.all_to_all(
        send.reshape(peers * halves, step_count, HD),
        ("dp", "tensor"),
        split_axis=0,
        concat_axis=0,
        tiled=True,
    )
    total = jnp.sum(got, axis=0)[:, : peers * capacity]
    return dec, total.T.reshape(1, peers * capacity, step_count)


def solution(mesh):
    in_specs = (
        P(("groups", "dp"), None, "tensor"),
        P(("groups", "dp"), None, None, "tensor"),
        P(("groups", "dp"), None, None, "tensor"),
        P(("groups", "dp"), None, None, "tensor"),
        P(("groups", "dp"), None, None, "tensor"),
        P(("groups", "dp")),
        P(("groups", "dp")),
        P(("groups", "dp")),
        P(("groups", "dp")),
        P("tensor"),
    )
    out_specs = (P(("groups", "dp"), None, "tensor"), P(("groups", "dp"), None, None))

    def run(*args):
        return per_device_ring(*args) if ring_fits(*args) else per_device(*args)

    return jax.shard_map(
        run, mesh=mesh, in_specs=in_specs, out_specs=out_specs, check_vma=False
    )
```

profile of v0, /device:TPU:0, one launch (start us, length us, event | category | flops | bytes accessed | tf_op | source)
XLA Modules:
  0.0 125.2 jit_solution(3419817241874052311)
XLA Ops:
  0.7 3.1 %collective-permute-start = (bf16[1,128,2,512]{3,2,1,0:T(2,128)(2,1)}, bf16[1,128,2,512]{3,2,1,0:T(2,128)(2,1)S(1)}, u32[]{:S(2)}, u32[]{:S(2)}) collective-permute-start(bf16[1,128,2,512]{3,2,1,0:T(2,128)(2,1)} %refs_8_.1), channel_id=1, source_target_pairs={{0,4},{4,8},{8,12},{12,14},{14,10},{10,6},{6,2},{2,0},{1,5},{5,9},... | collective-permute-start | bytes 786440 | tf_op jit(solution)/shard_map/ppermute | solution.py:609
  3.8 2.0 %collective-permute-start.8 = (bf16[1,128,2,512]{3,2,1,0:T(2,128)(2,1)}, bf16[1,128,2,512]{3,2,1,0:T(2,128)(2,1)S(1)}, u32[]{:S(2)}, u32[]{:S(2)}) collective-permute-start(bf16[1,128,2,512]{3,2,1,0:T(2,128)(2,1)} %refs_8_.1), channel_id=1, source_target_pairs={{4,0},{8,4},{12,8},{14,12},{10,14},{6,10},{2,6},{0,2},{5,1},{9,5},... | collective-permute-start | bytes 786440 | tf_op jit(solution)/shard_map/ppermute | solution.py:609
  5.8 5.3 %collective-permute-done.refs_8_ = bf16[1,128,2,512]{3,2,1,0:T(2,128)(2,1)S(1)} collective-permute-done((bf16[1,128,2,512]{3,2,1,0:T(2,128)(2,1)}, bf16[1,128,2,512]{3,2,1,0:T(2,128)(2,1)S(1)}, u32[]{:S(2)}, u32[]{:S(2)}) %collective-permute-start) | collective-permute-done | bytes 262176 | tf_op jit(solution)/shard_map/ppermute | solution.py:609
  11.1 2.1 %collective-permute-start.1 = (bf16[1,128,2,512]{3,2,1,0:T(2,128)(2,1)S(1)}, bf16[1,128,2,512]{3,2,1,0:T(2,128)(2,1)S(1)}, u32[]{:S(2)}, u32[]{:S(2)}) collective-permute-start(bf16[1,128,2,512]{3,2,1,0:T(2,128)(2,1)S(1)} %collective-permute-done.refs_8_), channel_id=1, source_target_pairs={{0,4},{4,8},{8,12},{12,14},{14,10},{10,6},{6,2},{2,0},{1,5},{5,9},... | collective-permute-start | bytes 786440 | tf_op jit(solution)/shard_map/ppermute | solution.py:609
  13.2 0.7 copy-done.8
  13.9 4.9 %collective-permute-done.8.refs_9_ = bf16[1,128,2,512]{3,2,1,0:T(2,128)(2,1)S(1)} collective-permute-done((bf16[1,128,2,512]{3,2,1,0:T(2,128)(2,1)}, bf16[1,128,2,512]{3,2,1,0:T(2,128)(2,1)S(1)}, u32[]{:S(2)}, u32[]{:S(2)}) %collective-permute-start.8) | collective-permute-done | bytes 262176 | tf_op jit(solution)/shard_map/ppermute | solution.py:609
  19.5 2.0 %collective-permute-start.12 = (bf16[1,128,2,512]{3,2,1,0:T(2,128)(2,1)S(1)}, bf16[1,128,2,512]{3,2,1,0:T(2,128)(2,1)}, u32[]{:S(2)}, u32[]{:S(2)}) collective-permute-start(bf16[1,128,2,512]{3,2,1,0:T(2,128)(2,1)S(1)} %collective-permute-done.11.refs_10_), channel_id=1, source_target_pairs={{0,4},{4,8},{8,12},{12,14},{14,10},{10,6},{6,2},{2,0},{1,5},{5,9},... | collective-permute-start | bytes 786440 | tf_op jit(solution)/shard_map/ppermute | solution.py:609
  21.5 0.7 copy-done.12
  22.3 2.1 %collective-permute-start.2 = (bf16[1,128,2,512]{3,2,1,0:T(2,128)(2,1)S(1)}, bf16[1,128,2,512]{3,2,1,0:T(2,128)(2,1)}, u32[]{:S(2)}, u32[]{:S(2)}) collective-permute-start(bf16[1,128,2,512]{3,2,1,0:T(2,128)(2,1)S(1)} %collective-permute-done.1.refs_8_), channel_id=1, source_target_pairs={{0,4},{4,8},{8,12},{12,14},{14,10},{10,6},{6,2},{2,0},{1,5},{5,9},... | collective-permute-start | bytes 786440 | tf_op jit(solution)/shard_map/ppermute | solution.py:609
  24.4 0.7 copy-done.14
  25.1 0.7 copy-done.16
  25.8 4.3 %collective-permute-done.9.refs_9_ = bf16[1,128,2,512]{3,2,1,0:T(2,128)(2,1)} collective-permute-done((bf16[1,128,2,512]{3,2,1,0:T(2,128)(2,1)S(1)}, bf16[1,128,2,512]{3,2,1,0:T(2,128)(2,1)}, u32[]{:S(2)}, u32[]{:S(2)}) %collective-permute-start.9) | collective-permute-done | bytes 262176 | tf_op jit(solution)/shard_map/ppermute | solution.py:609
  30.1 2.0 %collective-permute-start.13 = (bf16[1,128,2,512]{3,2,1,0:T(2,128)(2,1)}, bf16[1,128,2,512]{3,2,1,0:T(2,128)(2,1)}, u32[]{:S(2)}, u32[]{:S(2)}) collective-permute-start(bf16[1,128,2,512]{3,2,1,0:T(2,128)(2,1)} %collective-permute-done.12.refs_10_), channel_id=1, source_target_pairs={{0,4},{4,8},{8,12},{12,14},{14,10},{10,6},{6,2},{2,0},{1,5},{5,9},... | collective-permute-start | bytes 786440 | tf_op jit(solution)/shard_map/ppermute | solution.py:609
  32.1 2.2 %collective-permute-done.2.refs_8_ = bf16[1,128,2,512]{3,2,1,0:T(2,128)(2,1)} collective-permute-done((bf16[1,128,2,512]{3,2,1,0:T(2,128)(2,1)S(1)}, bf16[1,128,2,512]{3,2,1,0:T(2,128)(2,1)}, u32[]{:S(2)}, u32[]{:S(2)}) %collective-permute-start.2) | collective-permute-done | bytes 262176 | tf_op jit(solution)/shard_map/ppermute | solution.py:609
  34.4 2.0 %collective-permute-start.3 = (bf16[1,128,2,512]{3,2,1,0:T(2,128)(2,1)}, bf16[1,128,2,512]{3,2,1,0:T(2,128)(2,1)}, u32[]{:S(2)}, u32[]{:S(2)}) collective-permute-start(bf16[1,128,2,512]{3,2,1,0:T(2,128)(2,1)} %collective-permute-done.2.refs_8_), channel_id=1, source_target_pairs={{0,4},{4,8},{8,12},{12,14},{14,10},{10,6},{6,2},{2,0},{1,5},{5,9},... | collective-permute-start | bytes 786440 | tf_op jit(solution)/shard_map/ppermute | solution.py:609
  37.6 6.3 %all-to-all-start = ((s32[8,1,1]{2,1,0:T(1,128)}), s32[8,1,1]{2,1,0:T(1,128)S(1)}, u32[]{:S(2)}, u32[]{:S(2)}) async-start(s32[8,1,1]{2,1,0:T(1,128)} %broadcast_in_dim.8), calls=%async_computation | async-start | bytes 8192 | tf_op jit(solution)/shard_map/all_to_all | solution.py:615
  43.9 1.9 %slots.1.slot_ref.refs_3_ = s32[3,64]{1,0:T(4,128)} custom-call(s32[64]{0:T(128)} %owner_ref.1, s32[64]{0:T(128)} %len_ref.1, s32[64]{0:T(128)} %fin_ref.1), custom_call_target="tpu_custom_call" | custom-call | tf_op jit(solution)/shard_map/slots/pallas_call | solution.py:252
  45.8 1.6 %copy-done.2 = bf16[64,4,4096]{2,1,0:T(4,128)(2,1)S(1)} copy-done((bf16[64,4,4096]{2,1,0:T(4,128)(2,1)S(1)}, bf16[64,4,4096]{2,1,0:T(4,128)(2,1)}, u32[]{:S(2)}) %copy-start.2) | copy-done | bytes 2097176
  47.4 1.2 copy-done.3
  48.7 1.0 copy-done.4
  50.4 9.7 %prep.1 = (bf16[8,32,4096]{2,1,0:T(8,128)(2,1)S(1)}, bf16[8,128,512]{2,1,0:T(8,128)(2,1)S(1)}, bf16[8,128,512]{2,1,0:T(8,128)(2,1)S(1)}) custom-call(s32[3,64]{1,0:T(4,128)S(1)} %copy-done.19, bf16[64,4,4096]{2,1,0:T(4,128)(2,1)S(1)} %copy-done.2, bf16[64,8,2,512]{3,2,1,0:T(2,128)(2,1)S(1)} %copy-done.3, bf16[64,4,2,512]{3,2,1,0:T(2,128)(2,1)S(1)} %copy-done.4), custom_call_target="tpu_custom_call" | custom-call | bytes 12582912 | tf_op jit(solution)/shard_map/prep/pallas_call | solution.py:302
  60.2 6.2 %work.5 = (bf16[64,4,4096]{2,1,0:T(4,128)(2,1)}, f32[1,4,128]{2,1,0:T(4,128)S(1)}) custom-call(s32[1]{0:T(128)} %bitcast.refs_0_, s32[8,8]{1,0:T(8,128)S(1)} %copy-done.18, s32[1]{0:T(128)} %copy.21.refs_2_, s32[3,64]{1,0:T(4,128)S(1)} %copy-done.19, bf16[8,32,4096]{2,1,0:T(8,128)(2,1)S(1)} %get-tuple-element.15.refs_4_, ...), custom_call_target="tpu_custom_call" | custom-call | bytes 16777216 | tf_op jit(solution)/shard_map/work/pallas_call | solution.py:530
  66.4 1.0 copy-done
  67.6 1.2 copy-done.1
  68.8 0.9 copy-done.9
  69.8 0.9 copy-done.11
  70.7 0.9 copy-done.13
  71.7 11.1 %work.6 = (bf16[64,4,4096]{2,1,0:T(4,128)(2,1)}, f32[2,4,128]{2,1,0:T(4,128)S(1)}) custom-call(s32[1]{0:T(128)} %bitcast.refs_0_, s32[8,8]{1,0:T(8,128)S(1)} %copy-done.18, s32[8]{0:T(128)S(1)} %reduce.refs_2_, s32[3,64]{1,0:T(4,128)S(1)} %copy-done.20, bf16[8,32,4096]{2,1,0:T(8,128)(2,1)S(1)} %get-tuple-element.15.refs_4_, ...), custom_call_target="tpu_custom_call", output_to_operand_aliasing={{0}: (12, {})} | custom-call | bytes 16777216 | tf_op jit(solution)/shard_map/work/pallas_call | solution.py:530
  82.9 11.1 %work.7 = (bf16[64,4,4096]{2,1,0:T(4,128)(2,1)}, f32[2,4,128]{2,1,0:T(4,128)S(1)}) custom-call(s32[1]{0:T(128)} %bitcast.refs_0_, s32[8,8]{1,0:T(8,128)S(1)} %copy-done.18, s32[8]{0:T(128)S(1)} %reduce.refs_2_, s32[3,64]{1,0:T(4,128)S(1)} %copy-done.20, bf16[8,32,4096]{2,1,0:T(8,128)(2,1)S(1)} %get-tuple-element.15.refs_4_, ...), custom_call_target="tpu_custom_call", output_to_operand_aliasing={{0}: (12, {})} | custom-call | bytes 16777216 | tf_op jit(solution)/shard_map/work/pallas_call | solution.py:530
  94.0 11.2 %work.8 = (bf16[64,4,4096]{2,1,0:T(4,128)(2,1)}, f32[2,4,128]{2,1,0:T(4,128)S(1)}) custom-call(s32[1]{0:T(128)} %bitcast.refs_0_, s32[8,8]{1,0:T(8,128)S(1)} %copy-done.18, s32[8]{0:T(128)S(1)} %reduce.refs_2_, s32[3,64]{1,0:T(4,128)S(1)} %copy-done.20, bf16[8,32,4096]{2,1,0:T(8,128)(2,1)S(1)} %get-tuple-element.15.refs_4_, ...), custom_call_target="tpu_custom_call", output_to_operand_aliasing={{0}: (12, {})} | custom-call | bytes 16777216 | tf_op jit(solution)/shard_map/work/pallas_call | solution.py:530
  105.3 6.8 %work.9 = (bf16[64,4,4096]{2,1,0:T(4,128)(2,1)}, f32[8,2,4,128]{3,2,1,0:T(4,128)S(1)}) custom-call(s32[1]{0:T(128)} %bitcast.refs_0_, s32[8,8]{1,0:T(8,128)S(1)} %copy-done.18, s32[8]{0:T(128)S(1)} %reduce.refs_2_, s32[3,64]{1,0:T(4,128)S(1)} %copy-done.20, bf16[8,32,4096]{2,1,0:T(8,128)(2,1)S(1)} %get-tuple-element.15.refs_4_, ...), custom_call_target="tpu_custom_call", output_to_operand_aliasing={{0}: (10, {})} | custom-call | bytes 16777216 | tf_op jit(solution)/shard_map/work/pallas_call | solution.py:530
  112.1 12.5 %all_to_all.13 = f32[16,4,128]{2,1,0:T(4,128)S(1)} all-to-all(f32[16,4,128]{2,1,0:T(4,128)S(1)} %bitcast.14), channel_id=1, replica_groups=mesh['groups'=2,'dp'=8,'tensor'=2] {'dp','tensor'}, dimensions={0} | all-to-all | bytes 65536 | tf_op jit(solution)/shard_map/all_to_all | solution.py:642
  (52 shorter events, 3.1 us)
Async XLA Ops:
  0.6 59.5 %copy-start.18 = (s32[8,8]{1,0:T(8,128)S(1)}, s32[8,8]{1,0:T(8,128)}, u32[]{:S(2)}) copy-start(s32[8,8]{1,0:T(8,128)} %constant.10.clone.refs_1_) | copy-start | bytes 772
  0.6 59.5 %copy-start.5 = (f32[4096]{0:T(1024)S(1)}, f32[4096]{0:T(1024)}, u32[]{:S(2)}) copy-start(f32[4096]{0:T(1024)} %param.20) | copy-start | bytes 49156
  0.7 10.4 %collective-permute-start = (bf16[1,128,2,512]{3,2,1,0:T(2,128)(2,1)}, bf16[1,128,2,512]{3,2,1,0:T(2,128)(2,1)S(1)}, u32[]{:S(2)}, u32[]{:S(2)}) collective-permute-start(bf16[1,128,2,512]{3,2,1,0:T(2,128)(2,1)} %refs_8_.1), channel_id=1, source_target_pairs={{0,4},{4,8},{8,12},{12,14},{14,10},{10,6},{6,2},{2,0},{1,5},{5,9},... | collective-permute-start | bytes 786440 | tf_op jit(solution)/shard_map/ppermute | solution.py:609
  3.8 9.4 %collective-permute-start.4 = (bf16[1,128,2,512]{3,2,1,0:T(2,128)(2,1)}, bf16[1,128,2,512]{3,2,1,0:T(2,128)(2,1)S(1)}, u32[]{:S(2)}, u32[]{:S(2)}) collective-permute-start(bf16[1,128,2,512]{3,2,1,0:T(2,128)(2,1)} %refs_9_.1), channel_id=1, source_target_pairs={{4,0},{8,4},{12,8},{14,12},{10,14},{6,10},{2,6},{0,2},{5,1},{9,5},... | collective-permute-start | bytes 786440 | tf_op jit(solution)/shard_map/ppermute | solution.py:609
  3.8 15.0 %collective-permute-start.8 = (bf16[1,128,2,512]{3,2,1,0:T(2,128)(2,1)}, bf16[1,128,2,512]{3,2,1,0:T(2,128)(2,1)S(1)}, u32[]{:S(2)}, u32[]{:S(2)}) collective-permute-start(bf16[1,128,2,512]{3,2,1,0:T(2,128)(2,1)} %refs_8_.1), channel_id=1, source_target_pairs={{4,0},{8,4},{12,8},{14,12},{10,14},{6,10},{2,6},{0,2},{5,1},{9,5},... | collective-permute-start | bytes 786440 | tf_op jit(solution)/shard_map/ppermute | solution.py:609
  5.7 13.7 %collective-permute-start.11 = (bf16[1,128,2,512]{3,2,1,0:T(2,128)(2,1)}, bf16[1,128,2,512]{3,2,1,0:T(2,128)(2,1)S(1)}, u32[]{:S(2)}, u32[]{:S(2)}) collective-permute-start(bf16[1,128,2,512]{3,2,1,0:T(2,128)(2,1)} %refs_9_.1), channel_id=1, source_target_pairs={{0,4},{4,8},{8,12},{12,14},{14,10},{10,6},{6,2},{2,0},{1,5},{5,9},... | collective-permute-start | bytes 786440 | tf_op jit(solution)/shard_map/ppermute | solution.py:609
  11.1 11.2 %collective-permute-start.1 = (bf16[1,128,2,512]{3,2,1,0:T(2,128)(2,1)S(1)}, bf16[1,128,2,512]{3,2,1,0:T(2,128)(2,1)S(1)}, u32[]{:S(2)}, u32[]{:S(2)}) collective-permute-start(bf16[1,128,2,512]{3,2,1,0:T(2,128)(2,1)S(1)} %collective-permute-done.refs_8_), channel_id=1, source_target_pairs={{0,4},{4,8},{8,12},{12,14},{14,10},{10,6},{6,2},{2,0},{1,5},{5,9},... | collective-permute-start | bytes 786440 | tf_op jit(solution)/shard_map/ppermute | solution.py:609
  13.1 12.0 %collective-permute-start.5 = (bf16[1,128,2,512]{3,2,1,0:T(2,128)(2,1)S(1)}, bf16[1,128,2,512]{3,2,1,0:T(2,128)(2,1)S(1)}, u32[]{:S(2)}, u32[]{:S(2)}) collective-permute-start(bf16[1,128,2,512]{3,2,1,0:T(2,128)(2,1)S(1)} %collective-permute-done.4.refs_11_), channel_id=1, source_target_pairs={{4,0},{8,4},{12,8},{14,12},{10,14},{6,10},{2,6},{0,2},{5,1},{9,5},... | collective-permute-start | bytes 786440 | tf_op jit(solution)/shard_map/ppermute | solution.py:609
  18.8 11.3 %collective-permute-start.9 = (bf16[1,128,2,512]{3,2,1,0:T(2,128)(2,1)S(1)}, bf16[1,128,2,512]{3,2,1,0:T(2,128)(2,1)}, u32[]{:S(2)}, u32[]{:S(2)}) collective-permute-start(bf16[1,128,2,512]{3,2,1,0:T(2,128)(2,1)S(1)} %collective-permute-done.8.refs_9_), channel_id=1, source_target_pairs={{4,0},{8,4},{12,8},{14,12},{10,14},{6,10},{2,6},{0,2},{5,1},{9,5},... | collective-permute-start | bytes 786440 | tf_op jit(solution)/shard_map/ppermute | solution.py:609
  19.5 10.7 %collective-permute-start.12 = (bf16[1,128,2,512]{3,2,1,0:T(2,128)(2,1)S(1)}, bf16[1,128,2,512]{3,2,1,0:T(2,128)(2,1)}, u32[]{:S(2)}, u32[]{:S(2)}) collective-permute-start(bf16[1,128,2,512]{3,2,1,0:T(2,128)(2,1)S(1)} %collective-permute-done.11.refs_10_), channel_id=1, source_target_pairs={{0,4},{4,8},{8,12},{12,14},{14,10},{10,6},{6,2},{2,0},{1,5},{5,9},... | collective-permute-start | bytes 786440 | tf_op jit(solution)/shard_map/ppermute | solution.py:609
  22.3 12.1 %collective-permute-start.2 = (bf16[1,128,2,512]{3,2,1,0:T(2,128)(2,1)S(1)}, bf16[1,128,2,512]{3,2,1,0:T(2,128)(2,1)}, u32[]{:S(2)}, u32[]{:S(2)}) collective-permute-start(bf16[1,128,2,512]{3,2,1,0:T(2,128)(2,1)S(1)} %collective-permute-done.1.refs_8_), channel_id=1, source_target_pairs={{0,4},{4,8},{8,12},{12,14},{14,10},{10,6},{6,2},{2,0},{1,5},{5,9},... | collective-permute-start | bytes 786440 | tf_op jit(solution)/shard_map/ppermute | solution.py:609
  24.4 0.7 copy-start.14
  25.1 11.3 %collective-permute-start.6 = (bf16[1,128,2,512]{3,2,1,0:T(2,128)(2,1)S(1)}, bf16[1,128,2,512]{3,2,1,0:T(2,128)(2,1)}, u32[]{:S(2)}, u32[]{:S(2)}) collective-permute-start(bf16[1,128,2,512]{3,2,1,0:T(2,128)(2,1)S(1)} %collective-permute-done.5.refs_11_), channel_id=1, source_target_pairs={{4,0},{8,4},{12,8},{14,12},{10,14},{6,10},{2,6},{0,2},{5,1},{9,5},... | collective-permute-start | bytes 786440 | tf_op jit(solution)/shard_map/ppermute | solution.py:609
  25.1 0.7 copy-start.16
  30.1 63.9 %collective-permute-start.10 = (bf16[1,128,2,512]{3,2,1,0:T(2,128)(2,1)}, bf16[1,128,2,512]{3,2,1,0:T(2,128)(2,1)}, u32[]{:S(2)}, u32[]{:S(2)}) collective-permute-start(bf16[1,128,2,512]{3,2,1,0:T(2,128)(2,1)} %collective-permute-done.9.refs_9_), channel_id=1, source_target_pairs={{4,0},{8,4},{12,8},{14,12},{10,14},{6,10},{2,6},{0,2},{5,1},{9,5},... | collective-permute-start | bytes 786440 | tf_op jit(solution)/shard_map/ppermute | solution.py:609
  30.1 63.9 %collective-permute-start.13 = (bf16[1,128,2,512]{3,2,1,0:T(2,128)(2,1)}, bf16[1,128,2,512]{3,2,1,0:T(2,128)(2,1)}, u32[]{:S(2)}, u32[]{:S(2)}) collective-permute-start(bf16[1,128,2,512]{3,2,1,0:T(2,128)(2,1)} %collective-permute-done.12.refs_10_), channel_id=1, source_target_pairs={{0,4},{4,8},{8,12},{12,14},{14,10},{10,6},{6,2},{2,0},{1,5},{5,9},... | collective-permute-start | bytes 786440 | tf_op jit(solution)/shard_map/ppermute | solution.py:609
  34.4 70.9 %collective-permute-start.3 = (bf16[1,128,2,512]{3,2,1,0:T(2,128)(2,1)}, bf16[1,128,2,512]{3,2,1,0:T(2,128)(2,1)}, u32[]{:S(2)}, u32[]{:S(2)}) collective-permute-start(bf16[1,128,2,512]{3,2,1,0:T(2,128)(2,1)} %collective-permute-done.2.refs_8_), channel_id=1, source_target_pairs={{0,4},{4,8},{8,12},{12,14},{14,10},{10,6},{6,2},{2,0},{1,5},{5,9},... | collective-permute-start | bytes 786440 | tf_op jit(solution)/shard_map/ppermute | solution.py:609
  36.4 68.9 %collective-permute-start.7 = (bf16[1,128,2,512]{3,2,1,0:T(2,128)(2,1)}, bf16[1,128,2,512]{3,2,1,0:T(2,128)(2,1)}, u32[]{:S(2)}, u32[]{:S(2)}) collective-permute-start(bf16[1,128,2,512]{3,2,1,0:T(2,128)(2,1)} %collective-permute-done.6.refs_11_), channel_id=1, source_target_pairs={{4,0},{8,4},{12,8},{14,12},{10,14},{6,10},{2,6},{0,2},{5,1},{9,5},... | collective-permute-start | bytes 786440 | tf_op jit(solution)/shard_map/ppermute | solution.py:609
  37.6 29.7 %all-to-all-start = ((s32[8,1,1]{2,1,0:T(1,128)}), s32[8,1,1]{2,1,0:T(1,128)S(1)}, u32[]{:S(2)}, u32[]{:S(2)}) async-start(s32[8,1,1]{2,1,0:T(1,128)} %broadcast_in_dim.8), calls=%async_computation | async-start | bytes 8192 | tf_op jit(solution)/shard_map/all_to_all | solution.py:615
  45.8 1.6 %copy-start.2 = (bf16[64,4,4096]{2,1,0:T(4,128)(2,1)S(1)}, bf16[64,4,4096]{2,1,0:T(4,128)(2,1)}, u32[]{:S(2)}) copy-start(bf16[64,4,4096]{2,1,0:T(4,128)(2,1)} %x_hbm.1) | copy-start | bytes 6291460
  47.4 1.2 copy-start.3
  48.6 1.0 copy-start.4
  50.4 9.8 %copy-start.6 = (bf16[1,128,2,512]{3,2,1,0:T(2,128)(2,1)S(1)}, bf16[1,128,2,512]{3,2,1,0:T(2,128)(2,1)}, u32[]{:S(2)}) copy-start(bf16[1,128,2,512]{3,2,1,0:T(2,128)(2,1)} %refs_8_.1) | copy-start | bytes 786436
  50.4 9.8 %copy-start.7 = (bf16[1,128,2,512]{3,2,1,0:T(2,128)(2,1)S(1)}, bf16[1,128,2,512]{3,2,1,0:T(2,128)(2,1)}, u32[]{:S(2)}) copy-start(bf16[1,128,2,512]{3,2,1,0:T(2,128)(2,1)} %refs_9_.1) | copy-start | bytes 786436
  60.2 7.4 %copy-start.20 = (s32[3,64]{1,0:T(4,128)S(1)}, s32[3,64]{1,0:T(4,128)}, u32[]{:S(2)}) copy-start(s32[3,64]{1,0:T(4,128)} %slots.1.slot_ref.refs_3_) | copy-start | bytes 2308
  66.4 1.0 copy-start
  67.6 1.2 copy-start.1
  68.8 0.9 copy-start.9
  69.8 0.9 copy-start.11
  70.7 0.9 copy-start.13
  71.7 11.2 %copy-start.15 = (bf16[1,128,2,512]{3,2,1,0:T(2,128)(2,1)S(1)}, bf16[1,128,2,512]{3,2,1,0:T(2,128)(2,1)}, u32[]{:S(2)}) copy-start(bf16[1,128,2,512]{3,2,1,0:T(2,128)(2,1)} %copy-done.14) | copy-start | bytes 786436
  71.7 11.2 %copy-start.17 = (bf16[1,128,2,512]{3,2,1,0:T(2,128)(2,1)S(1)}, bf16[1,128,2,512]{3,2,1,0:T(2,128)(2,1)}, u32[]{:S(2)}) copy-start(bf16[1,128,2,512]{3,2,1,0:T(2,128)(2,1)} %copy-done.16) | copy-start | bytes 786436
  (4 other events, 2.8 us)
where the time goes:
time: 126 us; the launch traced here: 125 us
  Pallas kernels  58.2 us (46%)
  starting transfers between devices  21.7 us (17%)
  waiting for transfers between devices  16.8 us (13%)
  local copies, waits for them, and re-layouts  14.3 us (11%)
  blocking collectives  12.5 us (10%)
  between operations  1.5 us (1%)
    pallas_call x5, Pallas kernels, work_pieces(): pl.pallas_call(body, in_specs=specs, out_specs=[anyspec, vmem], out_shape...  46.5 us
    ppermute x14, waiting for transfers between devices, hop(): return lax.ppermute(value, 'dp', pairs)  16.8 us
    ppermute x14, starting transfers between devices, hop(): return lax.ppermute(value, 'dp', pairs)  15.4 us
    unnamed x42, local copies, waits for them, and re-layouts  13.1 us
    all_to_all x1, blocking collectives, per_device_ring(): lax.all_to_all(send.reshape(peers * halves, step_count, HD), ('dp', 'tens...  12.5 us
    pallas_call x1, Pallas kernels, prepare(): pl.pallas_call(prep_kernel, in_specs=[smem] + [anyspec] * 3, out_specs=[v...  9.75 us
    all_to_all x1, starting transfers between devices, per_device_ring(): lax.all_to_all(jnp.broadcast_to(prompt_len, (peers,)), 'dp', split_axis=0...  6.27 us
  transfers between devices with their start and end apart: 15, of which 5 were waited for; matrix products, arithmetic and copies ran while one was open for 1% of the time, Pallas kernels for 41%

commit v1 on v0

--- a/solution.py
+++ b/solution.py
@@ -67,9 +67,11 @@
     resp_values = own_all[:, :, 1].reshape(row_count, -1, kv_heads, HD)
     previous = jnp.zeros((row_count, q_width), jnp.float32)
     decoded_list = []
+    query_list = []
     kept_list = []
     for step_idx in range(step_count):
         queries = (step_input[:, step_idx].astype(jnp.float32) + previous).astype(jnp.bfloat16)
+        query_list.append(queries)
         received = lax.all_to_all(to_slots(queries), "dp", split_axis=0, concat_axis=0, tiled=True)
         lead_shape = received.shape[:2]
         prompt_queries = received.reshape(-1, kv_heads, group_size, HD)
@@ -196,6 +198,14 @@
     return list(range(0, count, 2)) + list(range(count - 1, 0, -2))
 
 
+def ring_owner(me, nth, count):
+    half = lax.div(me, 2)
+    spot = jnp.where(lax.rem(me, 2) == 0, half, count - 1 - half)
+    step = (nth + 1) // 2
+    spot = lax.rem(spot + (step if nth % 2 == 0 else count - step), count)
+    return jnp.where(spot < count // 2, 2 * spot, 2 * (count - 1 - spot) + 1)
+
+
 def iota(shape, dim):
     return lax.broadcasted_iota(jnp.int32, shape, dim)
 
@@ -257,67 +267,6 @@
         scratch_shapes=[pltpu.SMEM((peers,), jnp.int32)],
         name="slots",
     )(row_owner, resp_len, finished)
-
-
-def prep_kernel(slot_ref, x_hbm, rc_hbm, nk_hbm, xs_ref, ko_ref, vo_ref, xbuf, rcbuf, nkbuf, sem):
-    peers, width, kv_width = ko_ref.shape
-    _, capacity, old, _, _ = rcbuf.shape
-    steps = nkbuf.shape[2]
-    flights = []
-    for o in range(peers):
-        flight = []
-        for k in range(capacity):
-            row = jnp.maximum(slot_ref[0, o * capacity + k], 0)
-            flight += [
-                pltpu.make_async_copy(x_hbm.at[row], xbuf.at[o, k], sem.at[o, k, 0]),
-                pltpu.make_async_copy(rc_hbm.at[row], rcbuf.at[o, k], sem.at[o, k, 1]),
-                pltpu.make_async_copy(nk_hbm.at[row], nkbuf.at[o, k], sem.at[o, k, 2]),
-            ]
-        for c in flight:
-            c.start()
-        flights.append(flight)
-    n_old, n_new = capacity * old, capacity * steps
-    split_rc = split_matrix(n_old)
-    split_nk = split_matrix(n_new)
-    to_steps = swap_matrix(capacity, steps)
-    zero = jnp.zeros((width - n_old - n_new, kv_width), jnp.float32)
-    for o in range(peers):
-        for c in flights[o]:
-            c.wait()
-        rc = mm(split_rc, rcbuf[o].reshape(2 * n_old, kv_width))
-        nk = mm(split_nk, nkbuf[o].reshape(2 * n_new, kv_width))
-        ko_ref[o] = jnp.concatenate([rc[:n_old], nk[:n_new], zero], 0).astype(jnp.bfloat16)
-        vo_ref[o] = jnp.concatenate([rc[n_old:], nk[n_new:], zero], 0).astype(jnp.bfloat16)
-        xs_ref[o] = mm(to_steps, xbuf[o].reshape(n_new, -1)).astype(jnp.bfloat16)
-
-
-def prepare(slots, x, rc, nk, peers, capacity, width):
-    _, steps, q_width = x.shape
-    old = rc.shape[1]
-    kv_width = rc.shape[3]
-    smem = pl.BlockSpec(memory_space=pltpu.SMEM)
-    vmem = pl.BlockSpec(memory_space=pltpu.VMEM)
-    anyspec = pl.BlockSpec(memory_space=pl.ANY)
-    bf = jnp.bfloat16
-    return pl.pallas_call(
-        prep_kernel,
-        in_specs=[smem] + [anyspec] * 3,
-        out_specs=[vmem] * 3,
-        out_shape=[
-            jax.ShapeDtypeStruct((peers, steps * capacity, q_width), bf),
-            jax.ShapeDtypeStruct((peers, width, kv_width), bf),
-            jax.ShapeDtypeStruct((peers, width, kv_width), bf),
-        ],
-        scratch_shapes=[
-            pltpu.VMEM((peers, capacity, steps, q_width), bf),
-            pltpu.VMEM((peers, capacity, old, 2, kv_width), bf),
-            pltpu.VMEM((peers, capacity, steps, 2, kv_width), bf),
-            pltpu.SemaphoreType.DMA((peers, capacity, 3)),
-        ],
-        compiler_params=pltpu.CompilerParams(vmem_limit_bytes=24 << 20),
-        cost_estimate=pl.CostEstimate(flops=0, transcendentals=0, bytes_accessed=12 << 20),
-        name="prep",
-    )(slots, x, rc, nk)
 
 
 def own_masks(slot_ref, base, rows, old, steps, width):
@@ -336,105 +285,109 @@
     ]
 
 
-def make_work(pieces, begin, last, earlier, capacity, steps, old, kv_heads, group):
+def make_work(peers, pieces, begin, last, earlier, capacity, steps, old, kv_heads, group):
     head_rows = group * capacity
     inv_scale = 1.0 / math.sqrt(HD)
-    first = begin == 0
+    n_old, n_new = capacity * old, capacity * steps
 
     def body(*refs):
         refs = list(refs)
-        me_ref, table_ref, plen_ref, slot_ref = refs[:4]
-        xs_hbm, ko_hbm, vo_hbm, probe_ref = refs[4:8]
-        refs = refs[8:]
+        me_ref, slot_ref = refs[:2]
+        x_hbm, rc_hbm, nk_hbm, probe_ref = refs[2:6]
+        refs = refs[6:]
         pols, refs = refs[:pieces], refs[pieces:]
         rfs, refs = refs[:pieces], refs[pieces:]
-        if not first:
+        if begin > 0:
             refs = refs[1:]
         olds, refs = refs[:earlier], refs[earlier:]
         dec_hbm, score_ref = refs[:2]
-        polbuf, refbuf, xs, kc, vp, vr, obuf, insem, outsem = refs[2:]
+        polbuf, refbuf, xbuf, rcbuf, nkbuf, xs, kc, vc, qs, obuf, insem, rowsem, outsem = refs[2:]
         width = kc.shape[1] // 3
         kv_width = kv_heads * HD
         me = me_ref[0]
-        owners = [table_ref[me, begin + p] for p in range(pieces)]
-        loads = []
+        owners = [ring_owner(me, begin + p, peers) for p in range(pieces)]
+        loads, flights = [], []
         for p in range(pieces):
-            o = owners[p]
+            flight = []
+            for k in range(capacity):
+                row = jnp.maximum(slot_ref[0, owners[p] * capacity + k], 0)
+                flight += [
+                    pltpu.make_async_copy(x_hbm.at[row], xbuf.at[p, k], rowsem.at[p, k, 0]),
+                    pltpu.make_async_copy(rc_hbm.at[row], rcbuf.at[p, k], rowsem.at[p, k, 1]),
+                    pltpu.make_async_copy(nk_hbm.at[row], nkbuf.at[p, k], rowsem.at[p, k, 2]),
+                ]
+            flights.append(flight)
             loads.append(
                 [
                     pltpu.make_async_copy(pols[p].at[0], polbuf.at[p], insem.at[p, 0]),
                     pltpu.make_async_copy(rfs[p].at[0], refbuf.at[p], insem.at[p, 1]),
-                    pltpu.make_async_copy(xs_hbm.at[o], xs.at[p], insem.at[p, 2]),
-                    pltpu.make_async_copy(
-                        ko_hbm.at[o], kc.at[p, pl.ds(width, width)], insem.at[p, 3]
-                    ),
-                    pltpu.make_async_copy(
-                        vo_hbm.at[o], vr.at[p, pl.ds(width, width)], insem.at[p, 4]
-                    ),
                 ]
             )
-        for load in loads:
-            for c in load:
+        for p in range(pieces):
+            for c in flights[p] + loads[p]:
                 c.start()
         split_p = split_matrix(width)
+        split_rc = split_matrix(n_old)
+        split_nk = split_matrix(n_new)
+        to_steps = swap_matrix(capacity, steps)
         to_rows = swap_matrix(steps, capacity)
         masks = [
             own_masks(slot_ref, owners[p] * capacity, capacity, old, steps, width)
             for p in range(pieces)
         ]
-        lane = iota((head_rows, width), 1)
-        pmask = [lane < plen_ref[0 if first else owners[p]] for p in range(pieces)]
-        weights = [
-            jnp.concatenate(
-                [
-                    jnp.broadcast_to(
-                        probe_ref[g * group + h : g * group + h + 1, :], (capacity, HD)
-                    )
-                    for h in range(group)
-                ],
-                0,
-            )
-            for g in range(kv_heads)
-        ]
+        lane = iota((capacity, width), 1).astype(jnp.float32)
+        zero = jnp.zeros((width - n_old - n_new, kv_width), jnp.float32)
+        pmask = []
         for p in range(pieces):
+            for c in flights[p]:
+                c.wait()
+            rc = mm(split_rc, rcbuf[p].reshape(2 * n_old, kv_width))
+            nk = mm(split_nk, nkbuf[p].reshape(2 * n_new, kv_width))
+            own_k = jnp.concatenate([rc[:n_old], nk[:n_new], zero], 0).astype(jnp.bfloat16)
+            own_v = jnp.concatenate([rc[n_old:], nk[n_new:], zero], 0).astype(jnp.bfloat16)
+            kc[p, width : 2 * width] = own_k
+            vc[p, width : 2 * width] = own_v
+            xs[p] = mm(to_steps, xbuf[p].reshape(n_new, -1))
             for c in loads[p]:
                 c.wait()
             both = mm(split_p, polbuf[p].reshape(2 * width, kv_width)).astype(jnp.bfloat16)
             kc[p, :width] = both[:width]
-            vp[p] = both[width:]
-            both = mm(split_p, refbuf[p].reshape(2 * width, kv_width)).astype(jnp.bfloat16)
+            vc[p, :width] = both[width:]
+            both = mm(split_p, refbuf[p, :width].reshape(2 * width, kv_width)).astype(jnp.bfloat16)
             kc[p, 2 * width :] = both[:width]
-            vr[p, :width] = both[width:]
+            vc[p, 2 * width :] = both[width:]
+            length = refbuf[p, width].astype(jnp.float32)[:1, :width]
+            pmask.append(jnp.concatenate([lane < length] * group, 0))
         prev = [[None] * kv_heads for _ in range(pieces)]
         done = [[None] * steps for _ in range(pieces)]
-        totals = [[None] * steps for _ in range(pieces)]
         for s in range(steps):
             for p in range(pieces):
                 omask = jnp.concatenate([masks[p][s]] * group, 0)
-                x = xs[p, s * capacity : (s + 1) * capacity, :].astype(jnp.float32)
                 parts = []
-                total = jnp.zeros((head_rows, HD), jnp.float32)
                 for g in range(kv_heads):
                     at = slice(g * HD, (g + 1) * HD)
                     q = jnp.concatenate(
-                        [x[:, (g * group + h) * HD : (g * group + h + 1) * HD] for h in range(group)],
+                        [
+                            xs[p, s * capacity : (s + 1) * capacity, (g * group + h) * HD : (g * group + h + 1) * HD]
+                            for h in range(group)
+                        ],
                         0,
                     )
                     if s > 0:
                         q = q + prev[p][g]
                     q = q.astype(jnp.bfloat16)
-                    z = mm_t(q, kc[p, :, at]) * inv_scale
+                    qs[p, g, s * head_rows : (s + 1) * head_rows] = q
+                    z = mm_t(q, kc[p, : 2 * width, at]) * inv_scale
                     zp = jnp.where(pmask[p], z[:, :width], -jnp.inf)
-                    zo = jnp.where(omask, z[:, width : 2 * width], -jnp.inf)
-                    zr = jnp.where(pmask[p], z[:, 2 * width :], -jnp.inf)
+                    zo = jnp.where(omask, z[:, width:], -jnp.inf)
                     top_p = jnp.max(zp, axis=1, keepdims=True)
                     top_o = jnp.max(zo, axis=1, keepdims=True)
                     wp = jnp.exp(zp - top_p)
                     wo = jnp.exp(zo - top_o)
                     lp = jnp.sum(wp, axis=1, keepdims=True)
                     lo = jnp.sum(wo, axis=1, keepdims=True)
-                    accp = mm(wp.astype(jnp.bfloat16), vp[p, :, at])
-                    acco = mm(wo.astype(jnp.bfloat16), vr[p, width:, at])
+                    accp = mm(wp.astype(jnp.bfloat16), vc[p, :width, at])
+                    acco = mm(wo.astype(jnp.bfloat16), vc[p, width : 2 * width, at])
                     out_p = (accp * (1.0 / lp)).astype(jnp.bfloat16).astype(jnp.float32)
                     top = jnp.maximum(top_p, top_o)
                     a = lp * jnp.exp(top_p - top)
@@ -444,20 +397,7 @@
                     mix = mix.astype(jnp.bfloat16).astype(jnp.float32)
                     prev[p][g] = mix
                     parts += [mix[h * capacity : (h + 1) * capacity] for h in range(group)]
-                    top_r = jnp.maximum(jnp.max(zr, axis=1, keepdims=True), top_o)
-                    wr = jnp.exp(zr - top_r)
-                    wro = jnp.exp(zo - top_r)
-                    lr = jnp.sum(wr + wro, axis=1, keepdims=True)
-                    acc = mm(
-                        jnp.concatenate([wr.astype(jnp.bfloat16), wro.astype(jnp.bfloat16)], 1),
-                        vr[p, :, at],
-                    )
-                    total = total + (acc * (1.0 / lr)) * weights[g]
                 done[p][s] = jnp.concatenate(parts, 1)
-                fold = total[:capacity]
-                for h in range(1, group):
-                    fold = fold + total[h * capacity : (h + 1) * capacity]
-                totals[p][s] = fold
         for p in range(pieces):
             d = jnp.concatenate(done[p], 0).astype(jnp.bfloat16)
             obuf[p] = mm(to_rows, d).astype(jnp.bfloat16).reshape(obuf.shape[1:])
@@ -471,13 +411,33 @@
         out_lane = iota((capacity, HD), 1)
         out_sub = iota((capacity, HD), 0)
         for p in range(pieces):
+            full = jnp.concatenate(
+                [
+                    jnp.concatenate([jnp.concatenate([masks[p][s]] * group, 0), pmask[p]], 1)
+                    for s in range(steps)
+                ],
+                0,
+            )
+            total = [jnp.zeros((capacity, HD), jnp.float32) for _ in range(steps)]
+            for g in range(kv_heads):
+                at = slice(g * HD, (g + 1) * HD)
+                z = mm_t(qs[p, g], kc[p, width:, at]) * inv_scale
+                z = jnp.where(full, z, -jnp.inf)
+                w = jnp.exp(z - jnp.max(z, axis=1, keepdims=True))
+                acc = mm(w.astype(jnp.bfloat16), vc[p, width:, at])
+                acc = acc * (1.0 / jnp.sum(w, axis=1, keepdims=True))
+                for s in range(steps):
+                    for h in range(group):
+                        lo = (s * group + h) * capacity
+                        weight = probe_ref[g * group + h : g * group + h + 1, :]
+                        total[s] = total[s] + acc[lo : lo + capacity] * weight
             live = jnp.zeros((capacity, HD), jnp.int32)
             for k in range(capacity):
                 live = jnp.where(out_sub == k, slot_ref[2, owners[p] * capacity + k], live)
             here = (out_lane == me * capacity + out_sub) & (live == 1)
             rows = []
             for s in range(steps):
-                value = jnp.sum(totals[p][s], axis=1, keepdims=True)
+                value = jnp.sum(total[s], axis=1, keepdims=True)
                 rows.append(jnp.sum(jnp.where(here, value, 0.0), axis=0, keepdims=True))
             rows = jnp.concatenate(rows, 0)
             if last:
@@ -490,7 +450,7 @@
             for part in olds:
                 for i in range(part.shape[0]):
                     for t in range(score_ref.shape[1]):
-                        score_ref[table_ref[me, n], t] = part[i]
+                        score_ref[ring_owner(me, n, peers), t] = part[i]
                     n += 1
         for p in range(pieces):
             for k in range(capacity):
@@ -503,23 +463,24 @@
     return body
 
 
-def work_pieces(me, table, plen, slots, prep, probe, pols, rfs, dec, olds, shape, begin, last, old, halves):
+def work_pieces(me, peers, slots, rows, probe, pols, rfs, dec, olds, begin, last, halves):
+    x, rc, nk = rows
     pieces = len(pols)
-    first = begin == 0
-    xs, ko, vo = prep
-    _, steps, q_width = shape
-    peers, width, kv_width = ko.shape
-    capacity = xs.shape[1] // steps
+    _, steps, q_width = x.shape
+    _, width, _, kv_width = pols[0].shape
+    old = rc.shape[1]
+    capacity = slots.shape[1] // peers
     kv_heads = kv_width // HD
     group = q_width // kv_width
-    body = make_work(pieces, begin, last, len(olds), capacity, steps, old, kv_heads, group)
+    body = make_work(peers, pieces, begin, last, len(olds), capacity, steps, old, kv_heads, group)
     smem = pl.BlockSpec(memory_space=pltpu.SMEM)
     vmem = pl.BlockSpec(memory_space=pltpu.VMEM)
-    anyspec = pl.BlockSpec(memory_space=pl.ANY)
-    args = [me, table, plen, slots, xs, ko, vo, probe, *pols, *rfs]
-    specs = [smem] * 4 + [anyspec] * 3 + [vmem] + [anyspec] * (2 * pieces)
+    anyspec = pl.BlockSpec(memory_space=pltpu.HBM)
+    x, rc, nk = (pltpu.with_memory_space_constraint(v, pltpu.HBM) for v in rows)
+    args = [me, slots, x, rc, nk, probe, *pols, *rfs]
+    specs = [smem] * 2 + [anyspec] * 3 + [vmem] + [anyspec] * (2 * pieces)
     alias = {}
-    if not first:
+    if begin > 0:
         alias = {len(args): 0}
         args.append(dec)
         specs.append(anyspec)
@@ -532,18 +493,22 @@
         in_specs=specs,
         out_specs=[anyspec, vmem],
         out_shape=[
-            jax.ShapeDtypeStruct(shape, bf),
+            jax.ShapeDtypeStruct(x.shape, bf),
             jax.ShapeDtypeStruct(scores, jnp.float32),
         ],
         scratch_shapes=[
             pltpu.VMEM((pieces, width, 2, kv_width), bf),
-            pltpu.VMEM((pieces, width, 2, kv_width), bf),
-            pltpu.VMEM((pieces, capacity * steps, q_width), bf),
+            pltpu.VMEM((pieces, width + 1, 2, kv_width), bf),
+            pltpu.VMEM((pieces, capacity, steps, q_width), bf),
+            pltpu.VMEM((pieces, capacity, old, 2, kv_width), bf),
+            pltpu.VMEM((pieces, capacity, steps, 2, kv_width), bf),
+            pltpu.VMEM((pieces, capacity * steps, q_width), jnp.float32),
             pltpu.VMEM((pieces, 3 * width, kv_width), bf),
-            pltpu.VMEM((pieces, width, kv_width), bf),
-            pltpu.VMEM((pieces, 2 * width, kv_width), bf),
+            pltpu.VMEM((pieces, 3 * width, kv_width), bf),
+            pltpu.VMEM((pieces, kv_heads, steps * group * capacity, HD), bf),
             pltpu.VMEM((pieces, capacity, steps, q_width), bf),
-            pltpu.SemaphoreType.DMA((pieces, 5)),
+            pltpu.SemaphoreType.DMA((pieces, 2)),
+            pltpu.SemaphoreType.DMA((pieces, capacity, 3)),
             pltpu.SemaphoreType.DMA((pieces, capacity)),
         ],
         input_output_aliases=alias,
@@ -589,19 +554,10 @@
     row_count, step_count, q_width = step_input.shape
     peers = lax.axis_size("dp")
     halves = lax.axis_size("tensor")
-    width = policy_prompt.shape[1]
     capacity = max(2, (row_count + peers - 1) // peers)
-    old = resp_cache.shape[1]
     ring = ring_order(peers)
     forward = [(ring[i], ring[(i + 1) % peers]) for i in range(peers)]
     backward = [(b, a) for a, b in forward]
-    spot = {d: i for i, d in enumerate(ring)}
-    offsets = [0]
-    for d in range(1, peers // 2):
-        offsets += [-d, d]
-    offsets.append(peers // 2)
-    table = [[ring[(spot[dev] + off) % peers] for off in offsets] for dev in range(peers)]
-    table = jnp.array(table, jnp.int32)
     me = lax.axis_index("dp").astype(jnp.int32).reshape(1)
     probe_heads = probe.reshape(q_width // HD, HD)
 
@@ -610,22 +566,19 @@
 
     pf = hop(policy_prompt, forward)
     pb = hop(policy_prompt, backward)
-    rf = hop(ref_prompt, forward)
-    rb = hop(ref_prompt, backward)
-    plen_all = lax.all_to_all(
-        jnp.broadcast_to(prompt_len, (peers,)), "dp", split_axis=0, concat_axis=0, tiled=True
-    )
+    mark = jnp.broadcast_to(prompt_len.astype(jnp.bfloat16), (1, 1) + ref_prompt.shape[2:])
+    ref0 = jnp.concatenate([ref_prompt, mark], axis=1)
+    rf = hop(ref0, forward)
+    rb = hop(ref0, backward)
     slots = slot_tables(row_owner, resp_len, finished, peers, capacity)
-    prep = prepare(slots, step_input, resp_cache, new_kv, peers, capacity, width)
+    rows = (step_input, resp_cache, new_kv)
 
     def work(pols, rfs, dec, olds, begin, last=False):
-        plen = prompt_len if begin == 0 else plen_all
         return work_pieces(
-            me, table, plen, slots, prep, probe_heads, pols, rfs, dec, olds,
-            step_input.shape, begin, last, old, halves,
-        )
-
-    dec, score = work([policy_prompt], [ref_prompt], None, [], 0)
+            me, peers, slots, rows, probe_heads, pols, rfs, dec, olds, begin, last, halves
+        )
+
+    dec, score = work([policy_prompt], [ref0], None, [], 0)
     scores = [score]
     begin = 1
     for d in range(1, peers // 2):
@@ -637,7 +590,7 @@
         rb = hop(rb, backward)
         dec, score = work(*now, dec, [], begin)
         scores.append(score)
-        begin += 2
+        begin += len(now[0])
     dec, send = work([pf], [rb], dec, scores, begin, True)
     got = lax.all_to_all(
         send.reshape(peers * halves, step_count, HD),

time: 126 us -> 91 us (0.72)
  Pallas kernels: 58.2 us -> 34.7 us
  local copies, waits for them, and re-layouts: 14.3 us -> 4.08 us
  starting transfers between devices: 21.7 us -> 16.5 us
  waiting for transfers between devices: 16.8 us -> 21.1 us
    pallas_call x5, Pallas kernels: 46.5 us -> 32.8 us  [work_pieces(): pl.pallas_call(body, in_specs=specs, out_specs=[anyspec, vmem], out_shape...]
    unnamed x42 -> x6, local copies, waits for them, and re-layouts: 13.1 us -> 2.34 us
    pallas_call x1 -> x0, Pallas kernels: 9.75 us -> none  [prepare(): pl.pallas_call(prep_kernel, in_specs=[smem] + [anyspec] * 3, out_specs=[v...]
    all_to_all x1 -> x0, starting transfers between devices: 6.27 us -> none  [per_device_ring(): lax.all_to_all(jnp.broadcast_to(prompt_len, (peers,)), 'dp', split_axis=0...]
    ppermute x14, waiting for transfers between devices: 16.8 us -> 21.1 us  [hop(): return lax.ppermute(value, 'dp', pairs)]
  transfers between devices with their start and end apart: 15 -> 14, of which waited for: 5 -> 7; matrix products, arithmetic and copies ran while one was open for 1% -> 0% of each run, Pallas kernels for 41% -> 32%
where the time goes in v1:
time: 91 us; the launch traced here: 90.4 us
  Pallas kernels  34.7 us (38%)
  waiting for transfers between devices  21.1 us (23%)
  starting transfers between devices  16.5 us (18%)
  blocking collectives  12.5 us (14%)
  local copies, waits for them, and re-layouts  4.08 us (4%)
  between operations  1.39 us (2%)
    pallas_call x5, Pallas kernels, work_pieces(): pl.pallas_call(body, in_specs=specs, out_specs=[anyspec, vmem], out_shape...  32.8 us
    ppermute x14, waiting for transfers between devices, hop(): return lax.ppermute(value, 'dp', pairs)  21.1 us
    ppermute x14, starting transfers between devices, hop(): return lax.ppermute(value, 'dp', pairs)  16.5 us
    all_to_all x1, blocking collectives, per_device_ring(): lax.all_to_all(send.reshape(peers * halves, step_count, HD), ('dp', 'tens...  12.5 us
    unnamed x6, local copies, waits for them, and re-layouts  2.34 us
    pallas_call x1, Pallas kernels, slot_tables(): pl.pallas_call(slots_kernel, in_specs=[smem] * 3, out_specs=smem, out_sha...  1.91 us
  transfers between devices with their start and end apart: 14, of which 7 were waited for; matrix products, arithmetic and copies ran while one was open for 0% of the time, Pallas kernels for 32%

profile of v1, /device:TPU:0, one launch (start us, length us, event | category | flops | bytes accessed | tf_op | source)
XLA Modules:
  0.0 90.4 jit_solution(6269360454708860559)
XLA Ops:
  1.3 1.2 %concatenate.3.refs_7_ = bf16[1,129,2,512]{3,2,1,0:T(2,128)(2,1)S(1)} pad(bf16[1,128,2,512]{3,2,1,0:T(2,128)(2,1)} %param.14, bf16[]{:T(256)} %bitcast.2), padding=0_0x0_1x0_0x0_0 | pad | bytes 526338 | tf_op jit(solution)/shard_map/concatenate | solution.py:570
  2.4 3.0 %collective-permute-start.4 = (bf16[1,129,2,512]{3,2,1,0:T(2,128)(2,1)S(1)}, bf16[1,129,2,512]{3,2,1,0:T(2,128)(2,1)S(1)}, u32[]{:S(2)}, u32[]{:S(2)}) collective-permute-start(bf16[1,129,2,512]{3,2,1,0:T(2,128)(2,1)S(1)} %concatenate.3.refs_7_), channel_id=1, source_target_pairs={{4,0},{8,4},{12,8},{14,12},{10,14},{6,10},{2,6},{0,2},{5,1},{9,5},... | collective-permute-start | bytes 792584 | tf_op jit(solution)/shard_map/ppermute | solution.py:565
  5.5 0.1 collective-permute-start
  5.6 2.0 %collective-permute-start.11 = (bf16[1,129,2,512]{3,2,1,0:T(2,128)(2,1)S(1)}, bf16[1,129,2,512]{3,2,1,0:T(2,128)(2,1)S(1)}, u32[]{:S(2)}, u32[]{:S(2)}) collective-permute-start(bf16[1,129,2,512]{3,2,1,0:T(2,128)(2,1)S(1)} %concatenate.3.refs_7_), channel_id=1, source_target_pairs={{0,4},{4,8},{8,12},{12,14},{14,10},{10,6},{6,2},{2,0},{1,5},{5,9},... | collective-permute-start | bytes 792584 | tf_op jit(solution)/shard_map/ppermute | solution.py:565
  7.6 4.3 %collective-permute-done.4.refs_9_ = bf16[1,129,2,512]{3,2,1,0:T(2,128)(2,1)S(1)} collective-permute-done((bf16[1,129,2,512]{3,2,1,0:T(2,128)(2,1)S(1)}, bf16[1,129,2,512]{3,2,1,0:T(2,128)(2,1)S(1)}, u32[]{:S(2)}, u32[]{:S(2)}) %collective-permute-start.4) | collective-permute-done | bytes 264224 | tf_op jit(solution)/shard_map/ppermute | solution.py:565
  11.9 1.7 %collective-permute-start.5 = (bf16[1,129,2,512]{3,2,1,0:T(2,128)(2,1)S(1)}, bf16[1,129,2,512]{3,2,1,0:T(2,128)(2,1)S(1)}, u32[]{:S(2)}, u32[]{:S(2)}) collective-permute-start(bf16[1,129,2,512]{3,2,1,0:T(2,128)(2,1)S(1)} %collective-permute-done.4.refs_9_), channel_id=1, source_target_pairs={{4,0},{8,4},{12,8},{14,12},{10,14},{6,10},{2,6},{0,2},{5,1},{9,5},... | collective-permute-start | bytes 792584 | tf_op jit(solution)/shard_map/ppermute | solution.py:565
  13.6 1.6 %collective-permute-start.8 = (bf16[1,128,2,512]{3,2,1,0:T(2,128)(2,1)}, bf16[1,128,2,512]{3,2,1,0:T(2,128)(2,1)S(1)}, u32[]{:S(2)}, u32[]{:S(2)}) collective-permute-start(bf16[1,128,2,512]{3,2,1,0:T(2,128)(2,1)} %refs_6_.1), channel_id=1, source_target_pairs={{4,0},{8,4},{12,8},{14,12},{10,14},{6,10},{2,6},{0,2},{5,1},{9,5},... | collective-permute-start | bytes 786440 | tf_op jit(solution)/shard_map/ppermute | solution.py:565
  15.2 0.5 collective-permute-start.1
  15.6 4.9 %collective-permute-done.11.refs_8_ = bf16[1,129,2,512]{3,2,1,0:T(2,128)(2,1)S(1)} collective-permute-done((bf16[1,129,2,512]{3,2,1,0:T(2,128)(2,1)S(1)}, bf16[1,129,2,512]{3,2,1,0:T(2,128)(2,1)S(1)}, u32[]{:S(2)}, u32[]{:S(2)}) %collective-permute-start.11) | collective-permute-done | bytes 264224 | tf_op jit(solution)/shard_map/ppermute | solution.py:565
  20.5 0.1 collective-permute-start.12
  20.7 0.5 collective-permute-done.5.refs_9_
  21.1 1.7 %collective-permute-start.6 = (bf16[1,129,2,512]{3,2,1,0:T(2,128)(2,1)S(1)}, bf16[1,129,2,512]{3,2,1,0:T(2,128)(2,1)S(1)}, u32[]{:S(2)}, u32[]{:S(2)}) collective-permute-start(bf16[1,129,2,512]{3,2,1,0:T(2,128)(2,1)S(1)} %collective-permute-done.5.refs_9_), channel_id=1, source_target_pairs={{4,0},{8,4},{12,8},{14,12},{10,14},{6,10},{2,6},{0,2},{5,1},{9,5},... | collective-permute-start | bytes 792584 | tf_op jit(solution)/shard_map/ppermute | solution.py:565
  22.8 3.9 %collective-permute-done.8.refs_7_ = bf16[1,128,2,512]{3,2,1,0:T(2,128)(2,1)S(1)} collective-permute-done((bf16[1,128,2,512]{3,2,1,0:T(2,128)(2,1)}, bf16[1,128,2,512]{3,2,1,0:T(2,128)(2,1)S(1)}, u32[]{:S(2)}, u32[]{:S(2)}) %collective-permute-start.8) | collective-permute-done | bytes 262176 | tf_op jit(solution)/shard_map/ppermute | solution.py:565
  26.7 1.7 %collective-permute-start.9 = (bf16[1,128,2,512]{3,2,1,0:T(2,128)(2,1)S(1)}, bf16[1,128,2,512]{3,2,1,0:T(2,128)(2,1)S(1)}, u32[]{:S(2)}, u32[]{:S(2)}) collective-permute-start(bf16[1,128,2,512]{3,2,1,0:T(2,128)(2,1)S(1)} %collective-permute-done.8.refs_7_), channel_id=1, source_target_pairs={{4,0},{8,4},{12,8},{14,12},{10,14},{6,10},{2,6},{0,2},{5,1},{9,5},... | collective-permute-start | bytes 786440 | tf_op jit(solution)/shard_map/ppermute | solution.py:565
  28.4 0.3 collective-permute-start.2
  28.8 3.1 %collective-permute-done.12.refs_8_ = bf16[1,129,2,512]{3,2,1,0:T(2,128)(2,1)S(1)} collective-permute-done((bf16[1,129,2,512]{3,2,1,0:T(2,128)(2,1)S(1)}, bf16[1,129,2,512]{3,2,1,0:T(2,128)(2,1)S(1)}, u32[]{:S(2)}, u32[]{:S(2)}) %collective-permute-start.12) | collective-permute-done | bytes 264224 | tf_op jit(solution)/shard_map/ppermute | solution.py:565
  31.9 0.5 collective-permute-done.6.refs_9_
  32.4 1.7 %collective-permute-start.7 = (bf16[1,129,2,512]{3,2,1,0:T(2,128)(2,1)S(1)}, bf16[1,129,2,512]{3,2,1,0:T(2,128)(2,1)S(1)}, u32[]{:S(2)}, u32[]{:S(2)}) collective-permute-start(bf16[1,129,2,512]{3,2,1,0:T(2,128)(2,1)S(1)} %collective-permute-done.6.refs_9_), channel_id=1, source_target_pairs={{4,0},{8,4},{12,8},{14,12},{10,14},{6,10},{2,6},{0,2},{5,1},{9,5},... | collective-permute-start | bytes 792584 | tf_op jit(solution)/shard_map/ppermute | solution.py:565
  34.1 3.9 %collective-permute-done.9.refs_7_ = bf16[1,128,2,512]{3,2,1,0:T(2,128)(2,1)S(1)} collective-permute-done((bf16[1,128,2,512]{3,2,1,0:T(2,128)(2,1)S(1)}, bf16[1,128,2,512]{3,2,1,0:T(2,128)(2,1)S(1)}, u32[]{:S(2)}, u32[]{:S(2)}) %collective-permute-start.9) | collective-permute-done | bytes 262176 | tf_op jit(solution)/shard_map/ppermute | solution.py:565
  38.0 1.7 %collective-permute-start.10 = (bf16[1,128,2,512]{3,2,1,0:T(2,128)(2,1)S(1)}, bf16[1,128,2,512]{3,2,1,0:T(2,128)(2,1)}, u32[]{:S(2)}, u32[]{:S(2)}) collective-permute-start(bf16[1,128,2,512]{3,2,1,0:T(2,128)(2,1)S(1)} %collective-permute-done.9.refs_7_), channel_id=1, source_target_pairs={{4,0},{8,4},{12,8},{14,12},{10,14},{6,10},{2,6},{0,2},{5,1},{9,5},... | collective-permute-start | bytes 786440 | tf_op jit(solution)/shard_map/ppermute | solution.py:565
  39.7 0.3 collective-permute-start.3
  40.0 1.9 %slots.1.refs_1_ = s32[3,64]{1,0:T(4,128)} custom-call(s32[64]{0:T(128)} %owner_ref.1, s32[64]{0:T(128)} %len_ref.1, s32[64]{0:T(128)} %fin_ref.1), custom_call_target="tpu_custom_call" | custom-call | tf_op jit(solution)/shard_map/slots/pallas_call | solution.py:262
  42.0 0.7 copy-done
  42.7 0.9 %copy-done.1 = bf16[1,128,2,512]{3,2,1,0:T(2,128)(2,1)S(1)} copy-done((bf16[1,128,2,512]{3,2,1,0:T(2,128)(2,1)S(1)}, bf16[1,128,2,512]{3,2,1,0:T(2,128)(2,1)}, u32[]{:S(2)}) %copy-start.1) | copy-done | bytes 262168
  43.6 0.7 copy-done.2
  44.3 5.6 %work.5 = (bf16[64,4,4096]{2,1,0:T(4,128)(2,1)}, f32[1,4,128]{2,1,0:T(4,128)S(1)}) custom-call(s32[1]{0:T(128)} %bitcast.refs_0_, s32[3,64]{1,0:T(4,128)S(1)} %copy-done.2, bf16[64,4,4096]{2,1,0:T(4,128)(2,1)} %refs_2_.9, bf16[64,8,2,512]{3,2,1,0:T(2,128)(2,1)} %refs_3_.9, bf16[64,4,2,512]{3,2,1,0:T(2,128)(2,1)} %refs_4_.9, f32[32,128]{1,0:T(8,128)S(1)} %bitcast.8, ...), custom_call_target="tpu_custom_call" | custom-call | bytes 16777216 | tf_op jit(solution)/shard_map/work/pallas_call | solution.py:491
  49.9 7.2 %work.6 = (bf16[64,4,4096]{2,1,0:T(4,128)(2,1)}, f32[2,4,128]{2,1,0:T(4,128)S(1)}) custom-call(s32[1]{0:T(128)} %bitcast.refs_0_, s32[3,64]{1,0:T(4,128)S(1)} %copy-done.2, bf16[64,4,4096]{2,1,0:T(4,128)(2,1)} %refs_2_.9, bf16[64,8,2,512]{3,2,1,0:T(2,128)(2,1)} %refs_3_.9, bf16[64,4,2,512]{3,2,1,0:T(2,128)(2,1)} %refs_4_.9, ...), custom_call_target="tpu_custom_call", output_to_operand_aliasing={{0}: (10, {})} | custom-call | bytes 16777216 | tf_op jit(solution)/shard_map/work/pallas_call | solution.py:491
  57.1 7.2 %work.7 = (bf16[64,4,4096]{2,1,0:T(4,128)(2,1)}, f32[2,4,128]{2,1,0:T(4,128)S(1)}) custom-call(s32[1]{0:T(128)} %bitcast.refs_0_, s32[3,64]{1,0:T(4,128)S(1)} %copy-done.2, bf16[64,4,4096]{2,1,0:T(4,128)(2,1)} %refs_2_.9, bf16[64,8,2,512]{3,2,1,0:T(2,128)(2,1)} %refs_3_.9, bf16[64,4,2,512]{3,2,1,0:T(2,128)(2,1)} %refs_4_.9, ...), custom_call_target="tpu_custom_call", output_to_operand_aliasing={{0}: (10, {})} | custom-call | bytes 16777216 | tf_op jit(solution)/shard_map/work/pallas_call | solution.py:491
  64.3 7.2 %work.8 = (bf16[64,4,4096]{2,1,0:T(4,128)(2,1)}, f32[2,4,128]{2,1,0:T(4,128)S(1)}) custom-call(s32[1]{0:T(128)} %bitcast.refs_0_, s32[3,64]{1,0:T(4,128)S(1)} %copy-done.2, bf16[64,4,4096]{2,1,0:T(4,128)(2,1)} %refs_2_.9, bf16[64,8,2,512]{3,2,1,0:T(2,128)(2,1)} %refs_3_.9, bf16[64,4,2,512]{3,2,1,0:T(2,128)(2,1)} %refs_4_.9, ...), custom_call_target="tpu_custom_call", output_to_operand_aliasing={{0}: (10, {})} | custom-call | bytes 16777216 | tf_op jit(solution)/shard_map/work/pallas_call | solution.py:491
  71.6 5.6 %work.9 = (bf16[64,4,4096]{2,1,0:T(4,128)(2,1)}, f32[8,2,4,128]{3,2,1,0:T(4,128)S(1)}) custom-call(s32[1]{0:T(128)} %bitcast.refs_0_, s32[3,64]{1,0:T(4,128)S(1)} %copy-done.2, bf16[64,4,4096]{2,1,0:T(4,128)(2,1)} %refs_2_.9, bf16[64,8,2,512]{3,2,1,0:T(2,128)(2,1)} %refs_3_.9, bf16[64,4,2,512]{3,2,1,0:T(2,128)(2,1)} %refs_4_.9, ...), custom_call_target="tpu_custom_call", output_to_operand_aliasing={{0}: (8, {})} | custom-call | bytes 16777216 | tf_op jit(solution)/shard_map/work/pallas_call | solution.py:491
  77.2 12.5 %all_to_all.5 = f32[16,4,128]{2,1,0:T(4,128)S(1)} all-to-all(f32[16,4,128]{2,1,0:T(4,128)S(1)} %bitcast.13), channel_id=1, replica_groups=mesh['groups'=2,'dp'=8,'tensor'=2] {'dp','tensor'}, dimensions={0} | all-to-all | bytes 65536 | tf_op jit(solution)/shard_map/all_to_all | solution.py:595
  89.8 0.6 slice_bitcast_fusion
  (12 shorter events, 0.2 us)
Async XLA Ops:
  2.4 9.5 %collective-permute-start.4 = (bf16[1,129,2,512]{3,2,1,0:T(2,128)(2,1)S(1)}, bf16[1,129,2,512]{3,2,1,0:T(2,128)(2,1)S(1)}, u32[]{:S(2)}, u32[]{:S(2)}) collective-permute-start(bf16[1,129,2,512]{3,2,1,0:T(2,128)(2,1)S(1)} %concatenate.3.refs_7_), channel_id=1, source_target_pairs={{4,0},{8,4},{12,8},{14,12},{10,14},{6,10},{2,6},{0,2},{5,1},{9,5},... | collective-permute-start | bytes 792584 | tf_op jit(solution)/shard_map/ppermute | solution.py:565
  5.5 9.7 %collective-permute-start = (bf16[1,128,2,512]{3,2,1,0:T(2,128)(2,1)}, bf16[1,128,2,512]{3,2,1,0:T(2,128)(2,1)S(1)}, u32[]{:S(2)}, u32[]{:S(2)}) collective-permute-start(bf16[1,128,2,512]{3,2,1,0:T(2,128)(2,1)} %refs_6_.1), channel_id=1, source_target_pairs={{0,4},{4,8},{8,12},{12,14},{14,10},{10,6},{6,2},{2,0},{1,5},{5,9},... | collective-permute-start | bytes 786440 | tf_op jit(solution)/shard_map/ppermute | solution.py:565
  5.6 14.9 %collective-permute-start.11 = (bf16[1,129,2,512]{3,2,1,0:T(2,128)(2,1)S(1)}, bf16[1,129,2,512]{3,2,1,0:T(2,128)(2,1)S(1)}, u32[]{:S(2)}, u32[]{:S(2)}) collective-permute-start(bf16[1,129,2,512]{3,2,1,0:T(2,128)(2,1)S(1)} %concatenate.3.refs_7_), channel_id=1, source_target_pairs={{0,4},{4,8},{8,12},{12,14},{14,10},{10,6},{6,2},{2,0},{1,5},{5,9},... | collective-permute-start | bytes 792584 | tf_op jit(solution)/shard_map/ppermute | solution.py:565
  11.9 9.2 %collective-permute-start.5 = (bf16[1,129,2,512]{3,2,1,0:T(2,128)(2,1)S(1)}, bf16[1,129,2,512]{3,2,1,0:T(2,128)(2,1)S(1)}, u32[]{:S(2)}, u32[]{:S(2)}) collective-permute-start(bf16[1,129,2,512]{3,2,1,0:T(2,128)(2,1)S(1)} %collective-permute-done.4.refs_9_), channel_id=1, source_target_pairs={{4,0},{8,4},{12,8},{14,12},{10,14},{6,10},{2,6},{0,2},{5,1},{9,5},... | collective-permute-start | bytes 792584 | tf_op jit(solution)/shard_map/ppermute | solution.py:565
  13.6 13.2 %collective-permute-start.8 = (bf16[1,128,2,512]{3,2,1,0:T(2,128)(2,1)}, bf16[1,128,2,512]{3,2,1,0:T(2,128)(2,1)S(1)}, u32[]{:S(2)}, u32[]{:S(2)}) collective-permute-start(bf16[1,128,2,512]{3,2,1,0:T(2,128)(2,1)} %refs_6_.1), channel_id=1, source_target_pairs={{4,0},{8,4},{12,8},{14,12},{10,14},{6,10},{2,6},{0,2},{5,1},{9,5},... | collective-permute-start | bytes 786440 | tf_op jit(solution)/shard_map/ppermute | solution.py:565
  15.2 13.3 %collective-permute-start.1 = (bf16[1,128,2,512]{3,2,1,0:T(2,128)(2,1)S(1)}, bf16[1,128,2,512]{3,2,1,0:T(2,128)(2,1)S(1)}, u32[]{:S(2)}, u32[]{:S(2)}) collective-permute-start(bf16[1,128,2,512]{3,2,1,0:T(2,128)(2,1)S(1)} %collective-permute-done.refs_6_), channel_id=1, source_target_pairs={{0,4},{4,8},{8,12},{12,14},{14,10},{10,6},{6,2},{2,0},{1,5},{5,9},... | collective-permute-start | bytes 786440 | tf_op jit(solution)/shard_map/ppermute | solution.py:565
  20.5 11.3 %collective-permute-start.12 = (bf16[1,129,2,512]{3,2,1,0:T(2,128)(2,1)S(1)}, bf16[1,129,2,512]{3,2,1,0:T(2,128)(2,1)S(1)}, u32[]{:S(2)}, u32[]{:S(2)}) collective-permute-start(bf16[1,129,2,512]{3,2,1,0:T(2,128)(2,1)S(1)} %collective-permute-done.11.refs_8_), channel_id=1, source_target_pairs={{0,4},{4,8},{8,12},{12,14},{14,10},{10,6},{6,2},{2,0},{1,5},{5,9},... | collective-permute-start | bytes 792584 | tf_op jit(solution)/shard_map/ppermute | solution.py:565
  21.1 11.3 %collective-permute-start.6 = (bf16[1,129,2,512]{3,2,1,0:T(2,128)(2,1)S(1)}, bf16[1,129,2,512]{3,2,1,0:T(2,128)(2,1)S(1)}, u32[]{:S(2)}, u32[]{:S(2)}) collective-permute-start(bf16[1,129,2,512]{3,2,1,0:T(2,128)(2,1)S(1)} %collective-permute-done.5.refs_9_), channel_id=1, source_target_pairs={{4,0},{8,4},{12,8},{14,12},{10,14},{6,10},{2,6},{0,2},{5,1},{9,5},... | collective-permute-start | bytes 792584 | tf_op jit(solution)/shard_map/ppermute | solution.py:565
  26.7 11.3 %collective-permute-start.9 = (bf16[1,128,2,512]{3,2,1,0:T(2,128)(2,1)S(1)}, bf16[1,128,2,512]{3,2,1,0:T(2,128)(2,1)S(1)}, u32[]{:S(2)}, u32[]{:S(2)}) collective-permute-start(bf16[1,128,2,512]{3,2,1,0:T(2,128)(2,1)S(1)} %collective-permute-done.8.refs_7_), channel_id=1, source_target_pairs={{4,0},{8,4},{12,8},{14,12},{10,14},{6,10},{2,6},{0,2},{5,1},{9,5},... | collective-permute-start | bytes 786440 | tf_op jit(solution)/shard_map/ppermute | solution.py:565
  28.4 11.3 %collective-permute-start.2 = (bf16[1,128,2,512]{3,2,1,0:T(2,128)(2,1)S(1)}, bf16[1,128,2,512]{3,2,1,0:T(2,128)(2,1)S(1)}, u32[]{:S(2)}, u32[]{:S(2)}) collective-permute-start(bf16[1,128,2,512]{3,2,1,0:T(2,128)(2,1)S(1)} %collective-permute-done.1.refs_6_), channel_id=1, source_target_pairs={{0,4},{4,8},{8,12},{12,14},{14,10},{10,6},{6,2},{2,0},{1,5},{5,9},... | collective-permute-start | bytes 786440 | tf_op jit(solution)/shard_map/ppermute | solution.py:565
  31.8 32.5 %collective-permute-start.13 = (bf16[1,129,2,512]{3,2,1,0:T(2,128)(2,1)S(1)}, bf16[1,129,2,512]{3,2,1,0:T(2,128)(2,1)S(1)}, u32[]{:S(2)}, u32[]{:S(2)}) collective-permute-start(bf16[1,129,2,512]{3,2,1,0:T(2,128)(2,1)S(1)} %collective-permute-done.12.refs_8_), channel_id=1, source_target_pairs={{0,4},{4,8},{8,12},{12,14},{14,10},{10,6},{6,2},{2,0},{1,5},{5,9},... | collective-permute-start | bytes 792584 | tf_op jit(solution)/shard_map/ppermute | solution.py:565
  32.4 39.1 %collective-permute-start.7 = (bf16[1,129,2,512]{3,2,1,0:T(2,128)(2,1)S(1)}, bf16[1,129,2,512]{3,2,1,0:T(2,128)(2,1)S(1)}, u32[]{:S(2)}, u32[]{:S(2)}) collective-permute-start(bf16[1,129,2,512]{3,2,1,0:T(2,128)(2,1)S(1)} %collective-permute-done.6.refs_9_), channel_id=1, source_target_pairs={{4,0},{8,4},{12,8},{14,12},{10,14},{6,10},{2,6},{0,2},{5,1},{9,5},... | collective-permute-start | bytes 792584 | tf_op jit(solution)/shard_map/ppermute | solution.py:565
  38.0 26.3 %collective-permute-start.10 = (bf16[1,128,2,512]{3,2,1,0:T(2,128)(2,1)S(1)}, bf16[1,128,2,512]{3,2,1,0:T(2,128)(2,1)}, u32[]{:S(2)}, u32[]{:S(2)}) collective-permute-start(bf16[1,128,2,512]{3,2,1,0:T(2,128)(2,1)S(1)} %collective-permute-done.9.refs_7_), channel_id=1, source_target_pairs={{4,0},{8,4},{12,8},{14,12},{10,14},{6,10},{2,6},{0,2},{5,1},{9,5},... | collective-permute-start | bytes 786440 | tf_op jit(solution)/shard_map/ppermute | solution.py:565
  39.7 31.8 %collective-permute-start.3 = (bf16[1,128,2,512]{3,2,1,0:T(2,128)(2,1)S(1)}, bf16[1,128,2,512]{3,2,1,0:T(2,128)(2,1)}, u32[]{:S(2)}, u32[]{:S(2)}) collective-permute-start(bf16[1,128,2,512]{3,2,1,0:T(2,128)(2,1)S(1)} %collective-permute-done.2.refs_6_), channel_id=1, source_target_pairs={{0,4},{4,8},{8,12},{12,14},{14,10},{10,6},{6,2},{2,0},{1,5},{5,9},... | collective-permute-start | bytes 786440 | tf_op jit(solution)/shard_map/ppermute | solution.py:565
  42.0 0.7 copy-start
  42.7 0.9 %copy-start.1 = (bf16[1,128,2,512]{3,2,1,0:T(2,128)(2,1)S(1)}, bf16[1,128,2,512]{3,2,1,0:T(2,128)(2,1)}, u32[]{:S(2)}) copy-start(bf16[1,128,2,512]{3,2,1,0:T(2,128)(2,1)} %refs_6_.1) | copy-start | bytes 786436
  43.6 0.7 copy-start.2

commit v2 on v1

--- a/solution.py
+++ b/solution.py
@@ -67,11 +67,9 @@
     resp_values = own_all[:, :, 1].reshape(row_count, -1, kv_heads, HD)
     previous = jnp.zeros((row_count, q_width), jnp.float32)
     decoded_list = []
-    query_list = []
     kept_list = []
     for step_idx in range(step_count):
         queries = (step_input[:, step_idx].astype(jnp.float32) + previous).astype(jnp.bfloat16)
-        query_list.append(queries)
         received = lax.all_to_all(to_slots(queries), "dp", split_axis=0, concat_axis=0, tiled=True)
         lead_shape = received.shape[:2]
         prompt_queries = received.reshape(-1, kv_heads, group_size, HD)
@@ -233,9 +231,10 @@
     return lax.dot_general(a, b, (((1,), (1,)), ((), ())), preferred_element_type=jnp.float32)
 
 
-def slots_kernel(owner_ref, len_ref, fin_ref, slot_ref, count_ref):
+def slots_kernel(me_ref, owner_ref, len_ref, fin_ref, slot_ref, count_ref):
     peers = count_ref.shape[0]
     slots = slot_ref.shape[1]
+    slot_ref[3, 0] = me_ref[0]
     capacity = slots // peers
     for i in range(slots):
         slot_ref[0, i] = -1
@@ -257,16 +256,16 @@
     lax.fori_loop(0, owner_ref.shape[0], place, 0, unroll=4)
 
 
-def slot_tables(row_owner, resp_len, finished, peers, capacity):
+def slot_tables(me, row_owner, resp_len, finished, peers, capacity):
     smem = pl.BlockSpec(memory_space=pltpu.SMEM)
     return pl.pallas_call(
         slots_kernel,
-        in_specs=[smem] * 3,
+        in_specs=[smem] * 4,
         out_specs=smem,
-        out_shape=jax.ShapeDtypeStruct((3, peers * capacity), jnp.int32),
+        out_shape=jax.ShapeDtypeStruct((4, peers * capacity), jnp.int32),
         scratch_shapes=[pltpu.SMEM((peers,), jnp.int32)],
         name="slots",
-    )(row_owner, resp_len, finished)
+    )(me, row_owner, resp_len, finished)
 
 
 def own_masks(slot_ref, base, rows, old, steps, width):
@@ -292,19 +291,18 @@
 
     def body(*refs):
         refs = list(refs)
-        me_ref, slot_ref = refs[:2]
-        x_hbm, rc_hbm, nk_hbm, probe_ref = refs[2:6]
-        refs = refs[6:]
+        slot_ref, x_hbm, rc_hbm, nk_hbm, probe_hbm = refs[:5]
+        refs = refs[5:]
         pols, refs = refs[:pieces], refs[pieces:]
         rfs, refs = refs[:pieces], refs[pieces:]
         if begin > 0:
             refs = refs[1:]
         olds, refs = refs[:earlier], refs[earlier:]
         dec_hbm, score_ref = refs[:2]
-        polbuf, refbuf, xbuf, rcbuf, nkbuf, xs, kc, vc, qs, obuf, insem, rowsem, outsem = refs[2:]
+        probe_ref, polbuf, refbuf, xbuf, rcbuf, nkbuf, xs, kc, vc, qs, obuf, insem, rowsem, outsem, probesem = refs[2:]
         width = kc.shape[1] // 3
         kv_width = kv_heads * HD
-        me = me_ref[0]
+        me = slot_ref[3, 0]
         owners = [ring_owner(me, begin + p, peers) for p in range(pieces)]
         loads, flights = [], []
         for p in range(pieces):
@@ -326,6 +324,8 @@
         for p in range(pieces):
             for c in flights[p] + loads[p]:
                 c.start()
+        probe_load = pltpu.make_async_copy(probe_hbm, probe_ref, probesem)
+        probe_load.start()
         split_p = split_matrix(width)
         split_rc = split_matrix(n_old)
         split_nk = split_matrix(n_new)
@@ -408,6 +408,7 @@
                 def _():
                     pltpu.make_async_copy(obuf.at[p, k], dec_hbm.at[row], outsem.at[p, k]).start()
 
+        probe_load.wait()
         out_lane = iota((capacity, HD), 1)
         out_sub = iota((capacity, HD), 0)
         for p in range(pieces):
@@ -463,8 +464,8 @@
     return body
 
 
-def work_pieces(me, peers, slots, rows, probe, pols, rfs, dec, olds, begin, last, halves):
-    x, rc, nk = rows
+def work_pieces(peers, slots, rows, probe, pols, rfs, dec, olds, begin, last, halves):
+    x, rc, _ = rows
     pieces = len(pols)
     _, steps, q_width = x.shape
     _, width, _, kv_width = pols[0].shape
@@ -476,9 +477,12 @@
     smem = pl.BlockSpec(memory_space=pltpu.SMEM)
     vmem = pl.BlockSpec(memory_space=pltpu.VMEM)
     anyspec = pl.BlockSpec(memory_space=pltpu.HBM)
-    x, rc, nk = (pltpu.with_memory_space_constraint(v, pltpu.HBM) for v in rows)
-    args = [me, slots, x, rc, nk, probe, *pols, *rfs]
-    specs = [smem] * 2 + [anyspec] * 3 + [vmem] + [anyspec] * (2 * pieces)
+    big = [pltpu.with_memory_space_constraint(v, pltpu.HBM) for v in (*rows, probe)]
+    if begin == 0:
+        pols = [pltpu.with_memory_space_constraint(v, pltpu.HBM) for v in pols]
+    big += [*pols, *rfs]
+    args = [slots, *big]
+    specs = [smem] + [anyspec] * len(big)
     alias = {}
     if begin > 0:
         alias = {len(args): 0}
@@ -497,6 +501,7 @@
             jax.ShapeDtypeStruct(scores, jnp.float32),
         ],
         scratch_shapes=[
+            pltpu.VMEM(probe.shape, jnp.float32),
             pltpu.VMEM((pieces, width, 2, kv_width), bf),
             pltpu.VMEM((pieces, width + 1, 2, kv_width), bf),
             pltpu.VMEM((pieces, capacity, steps, q_width), bf),
@@ -510,6 +515,7 @@
             pltpu.SemaphoreType.DMA((pieces, 2)),
             pltpu.SemaphoreType.DMA((pieces, capacity, 3)),
             pltpu.SemaphoreType.DMA((pieces, capacity)),
+            pltpu.SemaphoreType.DMA,
         ],
         input_output_aliases=alias,
         compiler_params=pltpu.CompilerParams(vmem_limit_bytes=24 << 20),
@@ -570,12 +576,12 @@
     ref0 = jnp.concatenate([ref_prompt, mark], axis=1)
     rf = hop(ref0, forward)
     rb = hop(ref0, backward)
-    slots = slot_tables(row_owner, resp_len, finished, peers, capacity)
+    slots = slot_tables(me, row_owner, resp_len, finished, peers, capacity)
     rows = (step_input, resp_cache, new_kv)
 
     def work(pols, rfs, dec, olds, begin, last=False):
         return work_pieces(
-            me, peers, slots, rows, probe_heads, pols, rfs, dec, olds, begin, last, halves
+            peers, slots, rows, probe_heads, pols, rfs, dec, olds, begin, last, halves
         )
 
     dec, score = work([policy_prompt], [ref0], None, [], 0)

time: 91 us -> 87.3 us (0.959)
  Pallas kernels: 34.7 us -> 32.9 us
  local copies, waits for them, and re-layouts: 4.08 us -> 2.42 us
    pallas_call x5, Pallas kernels: 32.8 us -> 31 us  [work_pieces(): pl.pallas_call(body, in_specs=specs, out_specs=[anyspec, vmem], out_shape...]
    unnamed x6 -> x2, local copies, waits for them, and re-layouts: 2.34 us -> 0.68 us
where the time goes in v2:
time: 87.3 us; the launch traced here: 86.8 us
  Pallas kernels  32.9 us (38%)
  waiting for transfers between devices  21.1 us (24%)
  starting transfers between devices  16.5 us (19%)
  blocking collectives  12.5 us (14%)
  local copies, waits for them, and re-layouts  2.42 us (3%)
  between operations  1.39 us (2%)
    pallas_call x5, Pallas kernels, work_pieces(): pl.pallas_call(body, in_specs=specs, out_specs=[anyspec, vmem], out_shape...  31 us
    ppermute x14, waiting for transfers between devices, hop(): return lax.ppermute(value, 'dp', pairs)  21.1 us
    ppermute x14, starting transfers between devices, hop(): return lax.ppermute(value, 'dp', pairs)  16.5 us
    all_to_all x1, blocking collectives, per_device_ring(): lax.all_to_all(send.reshape(peers * halves, step_count, HD), ('dp', 'tens...  12.5 us
    pallas_call x1, Pallas kernels, slot_tables(): pl.pallas_call(slots_kernel, in_specs=[smem] * 4, out_specs=smem, out_sha...  1.91 us
  transfers between devices with their start and end apart: 14, of which 7 were waited for; matrix products, arithmetic and copies ran while one was open for 0% of the time, Pallas kernels for 32%

profile of v2, /device:TPU:0, one launch (start us, length us, event | category | flops | bytes accessed | tf_op | source)
XLA Modules:
  0.0 86.8 jit_solution(15747172397078276873)
XLA Ops:
  1.3 1.2 %concatenate.3.refs_6_ = bf16[1,129,2,512]{3,2,1,0:T(2,128)(2,1)S(1)} pad(bf16[1,128,2,512]{3,2,1,0:T(2,128)(2,1)} %param.14, bf16[]{:T(256)} %bitcast.2), padding=0_0x0_1x0_0x0_0 | pad | bytes 526338 | tf_op jit(solution)/shard_map/concatenate | solution.py:576
  2.4 3.0 %collective-permute-start.4 = (bf16[1,129,2,512]{3,2,1,0:T(2,128)(2,1)S(1)}, bf16[1,129,2,512]{3,2,1,0:T(2,128)(2,1)S(1)}, u32[]{:S(2)}, u32[]{:S(2)}) collective-permute-start(bf16[1,129,2,512]{3,2,1,0:T(2,128)(2,1)S(1)} %concatenate.3.refs_6_), channel_id=1, source_target_pairs={{4,0},{8,4},{12,8},{14,12},{10,14},{6,10},{2,6},{0,2},{5,1},{9,5},... | collective-permute-start | bytes 792584 | tf_op jit(solution)/shard_map/ppermute | solution.py:571
  5.5 0.1 collective-permute-start
  5.6 2.0 %collective-permute-start.11 = (bf16[1,129,2,512]{3,2,1,0:T(2,128)(2,1)S(1)}, bf16[1,129,2,512]{3,2,1,0:T(2,128)(2,1)S(1)}, u32[]{:S(2)}, u32[]{:S(2)}) collective-permute-start(bf16[1,129,2,512]{3,2,1,0:T(2,128)(2,1)S(1)} %concatenate.3.refs_6_), channel_id=1, source_target_pairs={{0,4},{4,8},{8,12},{12,14},{14,10},{10,6},{6,2},{2,0},{1,5},{5,9},... | collective-permute-start | bytes 792584 | tf_op jit(solution)/shard_map/ppermute | solution.py:571
  7.6 4.3 %collective-permute-done.4.refs_8_ = bf16[1,129,2,512]{3,2,1,0:T(2,128)(2,1)S(1)} collective-permute-done((bf16[1,129,2,512]{3,2,1,0:T(2,128)(2,1)S(1)}, bf16[1,129,2,512]{3,2,1,0:T(2,128)(2,1)S(1)}, u32[]{:S(2)}, u32[]{:S(2)}) %collective-permute-start.4) | collective-permute-done | bytes 264224 | tf_op jit(solution)/shard_map/ppermute | solution.py:571
  11.9 1.7 %collective-permute-start.5 = (bf16[1,129,2,512]{3,2,1,0:T(2,128)(2,1)S(1)}, bf16[1,129,2,512]{3,2,1,0:T(2,128)(2,1)S(1)}, u32[]{:S(2)}, u32[]{:S(2)}) collective-permute-start(bf16[1,129,2,512]{3,2,1,0:T(2,128)(2,1)S(1)} %collective-permute-done.4.refs_8_), channel_id=1, source_target_pairs={{4,0},{8,4},{12,8},{14,12},{10,14},{6,10},{2,6},{0,2},{5,1},{9,5},... | collective-permute-start | bytes 792584 | tf_op jit(solution)/shard_map/ppermute | solution.py:571
  13.6 1.6 %collective-permute-start.8 = (bf16[1,128,2,512]{3,2,1,0:T(2,128)(2,1)}, bf16[1,128,2,512]{3,2,1,0:T(2,128)(2,1)S(1)}, u32[]{:S(2)}, u32[]{:S(2)}) collective-permute-start(bf16[1,128,2,512]{3,2,1,0:T(2,128)(2,1)} %refs_5_.1), channel_id=1, source_target_pairs={{4,0},{8,4},{12,8},{14,12},{10,14},{6,10},{2,6},{0,2},{5,1},{9,5},... | collective-permute-start | bytes 786440 | tf_op jit(solution)/shard_map/ppermute | solution.py:571
  15.2 0.5 collective-permute-start.1
  15.6 4.9 %collective-permute-done.11.refs_7_ = bf16[1,129,2,512]{3,2,1,0:T(2,128)(2,1)S(1)} collective-permute-done((bf16[1,129,2,512]{3,2,1,0:T(2,128)(2,1)S(1)}, bf16[1,129,2,512]{3,2,1,0:T(2,128)(2,1)S(1)}, u32[]{:S(2)}, u32[]{:S(2)}) %collective-permute-start.11) | collective-permute-done | bytes 264224 | tf_op jit(solution)/shard_map/ppermute | solution.py:571
  20.5 0.1 collective-permute-start.12
  20.7 0.5 collective-permute-done.5.refs_8_
  21.1 1.7 %collective-permute-start.6 = (bf16[1,129,2,512]{3,2,1,0:T(2,128)(2,1)S(1)}, bf16[1,129,2,512]{3,2,1,0:T(2,128)(2,1)S(1)}, u32[]{:S(2)}, u32[]{:S(2)}) collective-permute-start(bf16[1,129,2,512]{3,2,1,0:T(2,128)(2,1)S(1)} %collective-permute-done.5.refs_8_), channel_id=1, source_target_pairs={{4,0},{8,4},{12,8},{14,12},{10,14},{6,10},{2,6},{0,2},{5,1},{9,5},... | collective-permute-start | bytes 792584 | tf_op jit(solution)/shard_map/ppermute | solution.py:571
  22.8 3.9 %collective-permute-done.8.refs_6_ = bf16[1,128,2,512]{3,2,1,0:T(2,128)(2,1)S(1)} collective-permute-done((bf16[1,128,2,512]{3,2,1,0:T(2,128)(2,1)}, bf16[1,128,2,512]{3,2,1,0:T(2,128)(2,1)S(1)}, u32[]{:S(2)}, u32[]{:S(2)}) %collective-permute-start.8) | collective-permute-done | bytes 262176 | tf_op jit(solution)/shard_map/ppermute | solution.py:571
  26.7 1.7 %collective-permute-start.9 = (bf16[1,128,2,512]{3,2,1,0:T(2,128)(2,1)S(1)}, bf16[1,128,2,512]{3,2,1,0:T(2,128)(2,1)S(1)}, u32[]{:S(2)}, u32[]{:S(2)}) collective-permute-start(bf16[1,128,2,512]{3,2,1,0:T(2,128)(2,1)S(1)} %collective-permute-done.8.refs_6_), channel_id=1, source_target_pairs={{4,0},{8,4},{12,8},{14,12},{10,14},{6,10},{2,6},{0,2},{5,1},{9,5},... | collective-permute-start | bytes 786440 | tf_op jit(solution)/shard_map/ppermute | solution.py:571
  28.4 0.3 collective-permute-start.2
  28.8 3.1 %collective-permute-done.12.refs_7_ = bf16[1,129,2,512]{3,2,1,0:T(2,128)(2,1)S(1)} collective-permute-done((bf16[1,129,2,512]{3,2,1,0:T(2,128)(2,1)S(1)}, bf16[1,129,2,512]{3,2,1,0:T(2,128)(2,1)S(1)}, u32[]{:S(2)}, u32[]{:S(2)}) %collective-permute-start.12) | collective-permute-done | bytes 264224 | tf_op jit(solution)/shard_map/ppermute | solution.py:571
  31.8 0.1 collective-permute-start.13
  31.9 0.5 collective-permute-done.6.refs_8_
  32.4 1.7 %collective-permute-start.7 = (bf16[1,129,2,512]{3,2,1,0:T(2,128)(2,1)S(1)}, bf16[1,129,2,512]{3,2,1,0:T(2,128)(2,1)S(1)}, u32[]{:S(2)}, u32[]{:S(2)}) collective-permute-start(bf16[1,129,2,512]{3,2,1,0:T(2,128)(2,1)S(1)} %collective-permute-done.6.refs_8_), channel_id=1, source_target_pairs={{4,0},{8,4},{12,8},{14,12},{10,14},{6,10},{2,6},{0,2},{5,1},{9,5},... | collective-permute-start | bytes 792584 | tf_op jit(solution)/shard_map/ppermute | solution.py:571
  34.1 3.9 %collective-permute-done.9.refs_6_ = bf16[1,128,2,512]{3,2,1,0:T(2,128)(2,1)S(1)} collective-permute-done((bf16[1,128,2,512]{3,2,1,0:T(2,128)(2,1)S(1)}, bf16[1,128,2,512]{3,2,1,0:T(2,128)(2,1)S(1)}, u32[]{:S(2)}, u32[]{:S(2)}) %collective-permute-start.9) | collective-permute-done | bytes 262176 | tf_op jit(solution)/shard_map/ppermute | solution.py:571
  38.0 1.7 %collective-permute-start.10 = (bf16[1,128,2,512]{3,2,1,0:T(2,128)(2,1)S(1)}, bf16[1,128,2,512]{3,2,1,0:T(2,128)(2,1)}, u32[]{:S(2)}, u32[]{:S(2)}) collective-permute-start(bf16[1,128,2,512]{3,2,1,0:T(2,128)(2,1)S(1)} %collective-permute-done.9.refs_6_), channel_id=1, source_target_pairs={{4,0},{8,4},{12,8},{14,12},{10,14},{6,10},{2,6},{0,2},{5,1},{9,5},... | collective-permute-start | bytes 786440 | tf_op jit(solution)/shard_map/ppermute | solution.py:571
  39.7 0.3 collective-permute-start.3
  40.0 1.9 %slots.1.refs_0_ = s32[4,64]{1,0:T(4,128)} custom-call(s32[1]{0:T(128)} %bitcast.me_ref, s32[64]{0:T(128)} %owner_ref.1, s32[64]{0:T(128)} %len_ref.1, s32[64]{0:T(128)} %fin_ref.1), custom_call_target="tpu_custom_call" | custom-call | tf_op jit(solution)/shard_map/slots/pallas_call | solution.py:261
  42.0 0.0 copy-start
  42.0 0.7 copy-done
  42.6 5.2 %work.5 = (bf16[64,4,4096]{2,1,0:T(4,128)(2,1)}, f32[1,4,128]{2,1,0:T(4,128)S(1)}) custom-call(s32[4,64]{1,0:T(4,128)S(1)} %copy-done, bf16[64,4,4096]{2,1,0:T(4,128)(2,1)} %refs_1_.9, bf16[64,8,2,512]{3,2,1,0:T(2,128)(2,1)} %refs_2_.9, bf16[64,4,2,512]{3,2,1,0:T(2,128)(2,1)} %refs_3_.9, f32[32,128]{1,0:T(8,128)} %bitcast.9, ...), custom_call_target="tpu_custom_call" | custom-call | bytes 16777216 | tf_op jit(solution)/shard_map/work/pallas_call | solution.py:495
  47.8 6.8 %work.6 = (bf16[64,4,4096]{2,1,0:T(4,128)(2,1)}, f32[2,4,128]{2,1,0:T(4,128)S(1)}) custom-call(s32[4,64]{1,0:T(4,128)S(1)} %copy-done, bf16[64,4,4096]{2,1,0:T(4,128)(2,1)} %refs_1_.9, bf16[64,8,2,512]{3,2,1,0:T(2,128)(2,1)} %refs_2_.9, bf16[64,4,2,512]{3,2,1,0:T(2,128)(2,1)} %refs_3_.9, f32[32,128]{1,0:T(8,128)} %bitcast.10, ...), custom_call_target="tpu_custom_call", output_to_operand_aliasing={{0}: (9, {})} | custom-call | bytes 16777216 | tf_op jit(solution)/shard_map/work/pallas_call | solution.py:495
  54.7 6.8 %work.7 = (bf16[64,4,4096]{2,1,0:T(4,128)(2,1)}, f32[2,4,128]{2,1,0:T(4,128)S(1)}) custom-call(s32[4,64]{1,0:T(4,128)S(1)} %copy-done, bf16[64,4,4096]{2,1,0:T(4,128)(2,1)} %refs_1_.9, bf16[64,8,2,512]{3,2,1,0:T(2,128)(2,1)} %refs_2_.9, bf16[64,4,2,512]{3,2,1,0:T(2,128)(2,1)} %refs_3_.9, f32[32,128]{1,0:T(8,128)} %bitcast.11, ...), custom_call_target="tpu_custom_call", output_to_operand_aliasing={{0}: (9, {})} | custom-call | bytes 16777216 | tf_op jit(solution)/shard_map/work/pallas_call | solution.py:495
  61.5 6.8 %work.8 = (bf16[64,4,4096]{2,1,0:T(4,128)(2,1)}, f32[2,4,128]{2,1,0:T(4,128)S(1)}) custom-call(s32[4,64]{1,0:T(4,128)S(1)} %copy-done, bf16[64,4,4096]{2,1,0:T(4,128)(2,1)} %refs_1_.9, bf16[64,8,2,512]{3,2,1,0:T(2,128)(2,1)} %refs_2_.9, bf16[64,4,2,512]{3,2,1,0:T(2,128)(2,1)} %refs_3_.9, f32[32,128]{1,0:T(8,128)} %bitcast.12, ...), custom_call_target="tpu_custom_call", output_to_operand_aliasing={{0}: (9, {})} | custom-call | bytes 16777216 | tf_op jit(solution)/shard_map/work/pallas_call | solution.py:495
  68.4 5.3 %work.9 = (bf16[64,4,4096]{2,1,0:T(4,128)(2,1)}, f32[8,2,4,128]{3,2,1,0:T(4,128)S(1)}) custom-call(s32[4,64]{1,0:T(4,128)S(1)} %copy-done, bf16[64,4,4096]{2,1,0:T(4,128)(2,1)} %refs_1_.9, bf16[64,8,2,512]{3,2,1,0:T(2,128)(2,1)} %refs_2_.9, bf16[64,4,2,512]{3,2,1,0:T(2,128)(2,1)} %refs_3_.9, f32[32,128]{1,0:T(8,128)} %bitcast.13, ...), custom_call_target="tpu_custom_call", output_to_operand_aliasing={{0}: (7, {})} | custom-call | bytes 16777216 | tf_op jit(solution)/shard_map/work/pallas_call | solution.py:495
  73.7 12.5 %all_to_all.5 = f32[16,4,128]{2,1,0:T(4,128)S(1)} all-to-all(f32[16,4,128]{2,1,0:T(4,128)S(1)} %bitcast.8), channel_id=1, replica_groups=mesh['groups'=2,'dp'=8,'tensor'=2] {'dp','tensor'}, dimensions={0} | all-to-all | bytes 65536 | tf_op jit(solution)/shard_map/all_to_all | solution.py:601
  86.3 0.6 slice_bitcast_fusion
  (8 shorter events, 0.0 us)
Async XLA Ops:
  2.4 9.5 %collective-permute-start.4 = (bf16[1,129,2,512]{3,2,1,0:T(2,128)(2,1)S(1)}, bf16[1,129,2,512]{3,2,1,0:T(2,128)(2,1)S(1)}, u32[]{:S(2)}, u32[]{:S(2)}) collective-permute-start(bf16[1,129,2,512]{3,2,1,0:T(2,128)(2,1)S(1)} %concatenate.3.refs_6_), channel_id=1, source_target_pairs={{4,0},{8,4},{12,8},{14,12},{10,14},{6,10},{2,6},{0,2},{5,1},{9,5},... | collective-permute-start | bytes 792584 | tf_op jit(solution)/shard_map/ppermute | solution.py:571
  5.5 9.7 %collective-permute-start = (bf16[1,128,2,512]{3,2,1,0:T(2,128)(2,1)}, bf16[1,128,2,512]{3,2,1,0:T(2,128)(2,1)S(1)}, u32[]{:S(2)}, u32[]{:S(2)}) collective-permute-start(bf16[1,128,2,512]{3,2,1,0:T(2,128)(2,1)} %refs_5_.1), channel_id=1, source_target_pairs={{0,4},{4,8},{8,12},{12,14},{14,10},{10,6},{6,2},{2,0},{1,5},{5,9},... | collective-permute-start | bytes 786440 | tf_op jit(solution)/shard_map/ppermute | solution.py:571
  5.6 14.9 %collective-permute-start.11 = (bf16[1,129,2,512]{3,2,1,0:T(2,128)(2,1)S(1)}, bf16[1,129,2,512]{3,2,1,0:T(2,128)(2,1)S(1)}, u32[]{:S(2)}, u32[]{:S(2)}) collective-permute-start(bf16[1,129,2,512]{3,2,1,0:T(2,128)(2,1)S(1)} %concatenate.3.refs_6_), channel_id=1, source_target_pairs={{0,4},{4,8},{8,12},{12,14},{14,10},{10,6},{6,2},{2,0},{1,5},{5,9},... | collective-permute-start | bytes 792584 | tf_op jit(solution)/shard_map/ppermute | solution.py:571
  11.9 9.2 %collective-permute-start.5 = (bf16[1,129,2,512]{3,2,1,0:T(2,128)(2,1)S(1)}, bf16[1,129,2,512]{3,2,1,0:T(2,128)(2,1)S(1)}, u32[]{:S(2)}, u32[]{:S(2)}) collective-permute-start(bf16[1,129,2,512]{3,2,1,0:T(2,128)(2,1)S(1)} %collective-permute-done.4.refs_8_), channel_id=1, source_target_pairs={{4,0},{8,4},{12,8},{14,12},{10,14},{6,10},{2,6},{0,2},{5,1},{9,5},... | collective-permute-start | bytes 792584 | tf_op jit(solution)/shard_map/ppermute | solution.py:571
  13.6 13.2 %collective-permute-start.8 = (bf16[1,128,2,512]{3,2,1,0:T(2,128)(2,1)}, bf16[1,128,2,512]{3,2,1,0:T(2,128)(2,1)S(1)}, u32[]{:S(2)}, u32[]{:S(2)}) collective-permute-start(bf16[1,128,2,512]{3,2,1,0:T(2,128)(2,1)} %refs_5_.1), channel_id=1, source_target_pairs={{4,0},{8,4},{12,8},{14,12},{10,14},{6,10},{2,6},{0,2},{5,1},{9,5},... | collective-permute-start | bytes 786440 | tf_op jit(solution)/shard_map/ppermute | solution.py:571
  15.2 13.3 %collective-permute-start.1 = (bf16[1,128,2,512]{3,2,1,0:T(2,128)(2,1)S(1)}, bf16[1,128,2,512]{3,2,1,0:T(2,128)(2,1)S(1)}, u32[]{:S(2)}, u32[]{:S(2)}) collective-permute-start(bf16[1,128,2,512]{3,2,1,0:T(2,128)(2,1)S(1)} %collective-permute-done.refs_5_), channel_id=1, source_target_pairs={{0,4},{4,8},{8,12},{12,14},{14,10},{10,6},{6,2},{2,0},{1,5},{5,9},... | collective-permute-start | bytes 786440 | tf_op jit(solution)/shard_map/ppermute | solution.py:571
  20.5 11.3 %collective-permute-start.12 = (bf16[1,129,2,512]{3,2,1,0:T(2,128)(2,1)S(1)}, bf16[1,129,2,512]{3,2,1,0:T(2,128)(2,1)S(1)}, u32[]{:S(2)}, u32[]{:S(2)}) collective-permute-start(bf16[1,129,2,512]{3,2,1,0:T(2,128)(2,1)S(1)} %collective-permute-done.11.refs_7_), channel_id=1, source_target_pairs={{0,4},{4,8},{8,12},{12,14},{14,10},{10,6},{6,2},{2,0},{1,5},{5,9},... | collective-permute-start | bytes 792584 | tf_op jit(solution)/shard_map/ppermute | solution.py:571
  21.1 11.3 %collective-permute-start.6 = (bf16[1,129,2,512]{3,2,1,0:T(2,128)(2,1)S(1)}, bf16[1,129,2,512]{3,2,1,0:T(2,128)(2,1)S(1)}, u32[]{:S(2)}, u32[]{:S(2)}) collective-permute-start(bf16[1,129,2,512]{3,2,1,0:T(2,128)(2,1)S(1)} %collective-permute-done.5.refs_8_), channel_id=1, source_target_pairs={{4,0},{8,4},{12,8},{14,12},{10,14},{6,10},{2,6},{0,2},{5,1},{9,5},... | collective-permute-start | bytes 792584 | tf_op jit(solution)/shard_map/ppermute | solution.py:571
  26.7 11.3 %collective-permute-start.9 = (bf16[1,128,2,512]{3,2,1,0:T(2,128)(2,1)S(1)}, bf16[1,128,2,512]{3,2,1,0:T(2,128)(2,1)S(1)}, u32[]{:S(2)}, u32[]{:S(2)}) collective-permute-start(bf16[1,128,2,512]{3,2,1,0:T(2,128)(2,1)S(1)} %collective-permute-done.8.refs_6_), channel_id=1, source_target_pairs={{4,0},{8,4},{12,8},{14,12},{10,14},{6,10},{2,6},{0,2},{5,1},{9,5},... | collective-permute-start | bytes 786440 | tf_op jit(solution)/shard_map/ppermute | solution.py:571
  28.4 11.3 %collective-permute-start.2 = (bf16[1,128,2,512]{3,2,1,0:T(2,128)(2,1)S(1)}, bf16[1,128,2,512]{3,2,1,0:T(2,128)(2,1)S(1)}, u32[]{:S(2)}, u32[]{:S(2)}) collective-permute-start(bf16[1,128,2,512]{3,2,1,0:T(2,128)(2,1)S(1)} %collective-permute-done.1.refs_5_), channel_id=1, source_target_pairs={{0,4},{4,8},{8,12},{12,14},{14,10},{10,6},{6,2},{2,0},{1,5},{5,9},... | collective-permute-start | bytes 786440 | tf_op jit(solution)/shard_map/ppermute | solution.py:571
  31.8 29.7 %collective-permute-start.13 = (bf16[1,129,2,512]{3,2,1,0:T(2,128)(2,1)S(1)}, bf16[1,129,2,512]{3,2,1,0:T(2,128)(2,1)S(1)}, u32[]{:S(2)}, u32[]{:S(2)}) collective-permute-start(bf16[1,129,2,512]{3,2,1,0:T(2,128)(2,1)S(1)} %collective-permute-done.12.refs_7_), channel_id=1, source_target_pairs={{0,4},{4,8},{8,12},{12,14},{14,10},{10,6},{6,2},{2,0},{1,5},{5,9},... | collective-permute-start | bytes 792584 | tf_op jit(solution)/shard_map/ppermute | solution.py:571
  32.4 36.0 %collective-permute-start.7 = (bf16[1,129,2,512]{3,2,1,0:T(2,128)(2,1)S(1)}, bf16[1,129,2,512]{3,2,1,0:T(2,128)(2,1)S(1)}, u32[]{:S(2)}, u32[]{:S(2)}) collective-permute-start(bf16[1,129,2,512]{3,2,1,0:T(2,128)(2,1)S(1)} %collective-permute-done.6.refs_8_), channel_id=1, source_target_pairs={{4,0},{8,4},{12,8},{14,12},{10,14},{6,10},{2,6},{0,2},{5,1},{9,5},... | collective-permute-start | bytes 792584 | tf_op jit(solution)/shard_map/ppermute | solution.py:571
  38.0 23.5 %collective-permute-start.10 = (bf16[1,128,2,512]{3,2,1,0:T(2,128)(2,1)S(1)}, bf16[1,128,2,512]{3,2,1,0:T(2,128)(2,1)}, u32[]{:S(2)}, u32[]{:S(2)}) collective-permute-start(bf16[1,128,2,512]{3,2,1,0:T(2,128)(2,1)S(1)} %collective-permute-done.9.refs_6_), channel_id=1, source_target_pairs={{4,0},{8,4},{12,8},{14,12},{10,14},{6,10},{2,6},{0,2},{5,1},{9,5},... | collective-permute-start | bytes 786440 | tf_op jit(solution)/shard_map/ppermute | solution.py:571
  39.7 28.7 %collective-permute-start.3 = (bf16[1,128,2,512]{3,2,1,0:T(2,128)(2,1)S(1)}, bf16[1,128,2,512]{3,2,1,0:T(2,128)(2,1)}, u32[]{:S(2)}, u32[]{:S(2)}) collective-permute-start(bf16[1,128,2,512]{3,2,1,0:T(2,128)(2,1)S(1)} %collective-permute-done.2.refs_5_), channel_id=1, source_target_pairs={{0,4},{4,8},{8,12},{12,14},{14,10},{10,6},{6,2},{2,0},{1,5},{5,9},... | collective-permute-start | bytes 786440 | tf_op jit(solution)/shard_map/ppermute | solution.py:571
  42.0 0.7 copy-start
